TPU v7x, 128 devices: a whole 4x4x4 slice. The times are simulated.
128 devices in a mesh: tile: 32 (over y, z, core), grp: 4 (over x).
Axes of the slice: x: 4, y: 4, z: 4, core: 2. Of those that a mesh axis runs over, the one named last changes fastest.
Arguments:
- soil_water: float32 [6, 8388608], P(None, ('tile', 'grp')), may hold values from 0.1 to 0.9
- rainfall: float32 [8388608], P(('tile', 'grp')), may hold values from 0.005 to 0.2
- drain_coef: float32 [6, 8388608], P(None, ('tile', 'grp')), may hold values from 0.02 to 0.5
- cell_storage: float32 [8388608], P(('tile', 'grp')), may hold values from 0.01 to 2
- release_rate: float32 [8388608], P(('tile', 'grp')), may hold values from 0.05 to 0.8
- downstream: int32 [8388608], P(('tile', 'grp')), may hold values from 1 to 128, as said below
- block_owner: int32 [65536, 1], P(('tile', 'grp')), may hold values from 0 to 127; in each aligned block of 512 rows (0 to 511, 512 to 1023, ...) at most 8 rows name the same one
- outlet_reach: int32 [65536], P(('tile', 'grp')), may hold values from 0 to 127
- river_storage: float32 [4, 4096], P('grp', 'tile'), may hold values from 0.02 to 0.5
- river_lag: float32 [4, 4096], P('grp', 'tile'), may hold values from 0 to 1
Outputs:
- soil_out: float32 [6, 8388608], P(None, ('tile', 'grp'))
- storage_out: float32 [8388608], P(('tile', 'grp'))
- section: float32 [4, 4096], P('grp', 'tile')
Inputs may be any that keep to these rules, and one draw needn't show every extreme that they name: `downstream`: within its block of 128 cells a cell drains to a later cell of the block, or to 128, the block's outlet. `block_owner`: of the 512 blocks of one device, at most 8 have the same owner.
All inputs are finite; a program needn't handle non-finite values.
Results may differ from a plain program's by a relative error of at most 0.0003.
Values sent between devices are 32-bit elements; how exact they have to be, the bound alone decides.
No kernel may reach another device: no remote copies, remote signals or barrier semaphores. Data moves between devices by JAX's collectives and lax.ppermute only.
A program may use at most 64 MiB of HBM per device.

v0:
```python
import jax
import jax.numpy as jnp
from jax import lax
from jax.experimental import pallas as pl
from jax.experimental.pallas import tpu as pltpu
from jax.sharding import PartitionSpec as P

SUB = 4
recharge_share = 0.2

W = 128
CHUNK = 128
FIELDS = 9
MB = 1024 * 1024


def gat(values, index):
    return jnp.take_along_axis(values, index, axis=1, mode="promise_in_bounds")


def iota(shape, dim):
    return lax.broadcasted_iota(jnp.int32, shape, dim)


def split3(x):
    hi = x.astype(jnp.bfloat16)
    rest = x - hi.astype(jnp.float32)
    mid = rest.astype(jnp.bfloat16)
    low = (rest - mid.astype(jnp.float32)).astype(jnp.bfloat16)
    return hi, mid, low


def pick(onehot, x):
    hi, mid, low = split3(x)
    dot = lambda part: jnp.dot(onehot, part, preferred_element_type=jnp.float32)
    return dot(hi) + dot(mid) + dot(low)


def moments_kernel(
    soil, coef, rain, storage, rate, links, owner, reach, send, packed, carry
):
    step = pl.program_id(0)
    lane = iota((CHUNK, W), 1)
    sub = iota((CHUNK, W), 0)
    own = jnp.broadcast_to(owner[pl.ds(step, 1), :], (W, CHUNK))
    hit = (own == sub).astype(jnp.float32)
    hit16 = hit.astype(jnp.bfloat16)

    @pl.when(step == 0)
    def _():
        send[...] = jnp.zeros_like(send)
        carry[...] = jnp.zeros_like(carry)

    before = (sub < lane).astype(jnp.bfloat16)
    seen = jnp.dot(hit16, before, preferred_element_type=jnp.float32) + carry[...]
    carry[...] += jnp.sum(hit, axis=1, keepdims=True)
    rank = jnp.sum(hit * seen, axis=0, keepdims=True)
    both = rank + 8.0 * reach[pl.ds(step, 1), :].astype(jnp.float32)
    both = jnp.transpose(jnp.broadcast_to(both, (W, CHUNK))).astype(jnp.int32)
    packed[...] = both.astype(jnp.float32)

    rows = 32

    def body(i, _):
        at = pl.ds(pl.multiple_of(i * rows, rows), rows)
        w0, w5, c5 = soil[at, 0, :], soil[at, 5, :], coef[at, 5, :]
        s, r, down = storage[at, :], rate[at, :], links[at, :]
        share = (rain[at, :] * w0 * w0 + c5 * w5 * w5 * w5) * (1.0 / SUB)
        leaves = down == W
        to = down & (W - 1)
        follow = lambda v: jnp.where(leaves, 0.0, gat(v, to))
        a1 = jnp.where(leaves, r, 0.0)
        a2 = a1 * r
        a3 = a2 * r
        g = follow(a1)
        w_1 = r * g
        w_2 = w_1 * g
        w_3 = w_2 * g
        x_1 = r * follow(w_1)
        x_2 = r * follow(w_2)
        z = w_1 * (1.0 - r) + x_1
        y = r * follow(z)
        e1 = (1.0 - r) * s + share
        h1 = a1 * share
        h2 = a2 * share
        terms = (
            a1 * s,
            a2 * s,
            a3 * s,
            a3 * r * s,
            h1 + w_1 * s,
            h2 + w_2 * s,
            a3 * share + w_3 * s,
            h1 + w_1 * e1 + x_1 * s,
            h2 + w_2 * e1 + x_2 * s,
            h1 + w_1 * share + z * e1 + y * s,
        )
        lane = iota((rows, W), 1)
        field = lane & 15
        both = packed[at, :].astype(jnp.int32)
        out = (both >> 3).astype(jnp.float32)
        for f, term in enumerate(terms):
            out = jnp.where(field == f, jnp.sum(term, axis=1, keepdims=True), out)
        packed[at, :] = jnp.where((lane >> 4) == (both & 7), out, 0.0)
        return 0

    lax.fori_loop(0, CHUNK // rows, body, 0)
    send[...] += pick(hit16, packed[...])


def inflow_kernel(soil, coef, rain, storage, rate, links, owner, reach, soil_mid, gains, hit, spot):
    step = pl.program_id(0)
    rows = 32
    sub = iota((CHUNK, W), 0)
    own = jnp.broadcast_to(owner[pl.ds(step, 1), :], (W, CHUNK))
    hit[...] = jnp.transpose((own == sub).astype(jnp.float32)).astype(jnp.bfloat16)
    at_reach = jnp.broadcast_to(reach[pl.ds(step, 1), :].astype(jnp.float32), (W, CHUNK))
    spot[...] = jnp.transpose(at_reach).astype(jnp.int32)

    def body(i, _):
        at = pl.ds(pl.multiple_of(i * rows, rows), rows)
        lane = iota((rows, W), 1)
        rainfall = rain[at, :]
        w0 = soil[at, 0, :]
        surface = rainfall * w0 * w0
        coming = rainfall - surface
        for layer in range(6):
            water = soil[at, layer, :]
            drained = coef[at, layer, :] * water * water * water
            soil_mid[at, layer, :] = water + coming - drained
            coming = drained
        share = (surface + coming) * (1.0 / SUB)

        down = links[at, :]
        key = (down * W + lane).astype(jnp.float32)
        size = 2
        while size <= W:
            j = size // 2
            while j >= 1:
                other = gat(key, lane ^ j)
                low = ((lane & j) == 0) == ((lane & size) == 0)
                key = jnp.where(low, jnp.minimum(key, other), jnp.maximum(key, other))
                j //= 2
            size *= 2
        key = key.astype(jnp.int32)
        order = key & (W - 1)
        dest = key >> 7
        same = []
        shift = 1
        while shift < W:
            linked = (lane >= shift) & (dest == pltpu.roll(dest, shift, 1))
            same.append((shift, linked.astype(jnp.float32)))
            shift *= 2
        count = jnp.zeros((rows, W), jnp.int32)
        for shift in (64, 32, 16, 8, 4, 2, 1):
            nxt = count + shift
            count = jnp.where(gat(dest, nxt - 1) <= lane, nxt, count)
        end = jnp.maximum(count - 1, 0)
        fed = (count > 0) & (gat(dest, end) == lane)

        s, r = storage[at, :], rate[at, :]
        for n in range(SUB):
            release = r * s
            run = gat(release, order)
            for shift, linked in same:
                run = run + linked * pltpu.roll(run, shift, 1)
            gain = share + jnp.where(fed, gat(run, end), 0.0)
            gains[n, at, :] = gain
            s = s + gain - release
        return 0

    lax.fori_loop(0, CHUNK // rows, body, 0)


def reach_kernel(recv, volume, lag, out):
    got = recv[...]
    turned = jnp.transpose(got)
    lane = iota((W, W), 1)
    total = jnp.zeros((16, W), jnp.float32)
    for c in range(8):
        at = got[:, c * 16 + 10 : c * 16 + 11].astype(jnp.int32)
        hit = (at == lane).astype(jnp.bfloat16)
        for part in split3(turned[c * 16 : c * 16 + 16, :]):
            total += jnp.dot(part, hit, preferred_element_type=jnp.float32)
    row = lambda f: total[f : f + 1, :]
    vol = volume[...]
    back = 1.0 / (1.0 + vol)
    lateral = back * row(0) * (1.0 / W)
    s1 = row(0) - back * row(1) + row(4)
    s2 = row(1) - back * row(2) + row(5)
    s3 = row(2) - back * row(3) + row(6)
    fields = (lag[...], vol, lateral, s1, s2, s3, row(7), row(8), row(9))
    for f, value in enumerate(fields):
        out[:, f * W : (f + 1) * W] = jnp.broadcast_to(value, (W, W))


def shift_rows(x, by, fill):
    return jnp.concatenate([jnp.full((by, W), fill, x.dtype), x[:-by, :]], axis=0)


def finish_kernel(
    me, fields, gains, storage, rate, links, hit, spot, soil_mid, soil_out, storage_out, section, table, flow_ref
):
    lane = iota((W, W), 1)

    @pl.when(pl.program_id(0) == 0)
    def _():
        field = lambda f: fields[:, f * W : (f + 1) * W]
        lag = field(0)
        weight = 1.0 / (1.0 + lag)
        stages = []
        base = weight
        total = weight
        stride = 1
        for radix in (4, 4, 8):
            shifted = [base]
            neutral = total
            gains_of = []
            product = base
            for d in range(1, radix):
                ok = lane >= d * stride
                gains_of.append((d * stride, jnp.where(ok, product, 0.0)))
                moved = pltpu.roll(base, d * stride, 1)
                product = product * moved
                neutral = neutral * jnp.where(ok, pltpu.roll(total, d * stride, 1), 1.0)
            stages.append(gains_of)
            base, total = product, neutral
            stride *= radix
        last = jnp.broadcast_to(total[:, W - 1 : W], (W, W))
        hops = []
        jump = last
        by = 4
        while by < W:
            hops.append((by, jump))
            jump = jump * shift_rows(jump, by, 0.0)
            by *= 2

        volume = field(1)
        lateral = field(2)
        s1, s2, s3 = field(3), field(4), field(5)
        c11, c12, c21 = field(6), field(7), field(8)
        flow = volume
        for n in range(SUB):
            back = 1.0 / (1.0 + volume)
            for part, value in enumerate(split3(back)):
                table[:, (part * SUB + n) * W : (part * SUB + n + 1) * W] = value
            if n == 1:
                lateral = back * s1 * (1.0 / W)
                s1, s2 = s1 - back * s2 + c11, s2 - back * s3 + c12
            elif n == 2:
                lateral = back * s1 * (1.0 / W)
                s1 = s1 - back * s2 + c21
            elif n == 3:
                lateral = back * s1 * (1.0 / W)
            run = weight * (volume + lateral)
            for gains_of in stages:
                add = run
                for d, gain in gains_of:
                    add = add + gain * pltpu.roll(run, d, 1)
                run = add
            head = jnp.broadcast_to(run[:, W - 1 : W], (W, W))
            for by, jump in hops:
                head = head + jump * shift_rows(head, by, 0.0)
            flow = run + total * shift_rows(head, 4, 0.0)
            volume = lag * flow
        flow_ref[...] = flow
        section[...] = jnp.log1p(flow_ref[pl.ds(me[0], 1), :])

    rows = 64
    for half in range(CHUNK // rows):
        at = slice(half * rows, (half + 1) * rows)
        got = jnp.dot(hit[at, :], table[...], preferred_element_type=jnp.float32)
        place = spot[at, :]
        s, r = storage[at, :], rate[at, :]
        leaves = links[at, :] == W
        for n in range(SUB):
            part = lambda k: got[:, (k * SUB + n) * W : (k * SUB + n + 1) * W]
            back = gat(part(0) + part(1) + part(2), place)
            s = s - r * jnp.where(leaves, back, 1.0) * s + gains[n, at, :]
        storage_out[at, :] = s
        top = soil_mid[at, 0, :]
        soil_out[at, 0, :] = top + recharge_share * (s / (s + 1.0)) * (1.0 - top)
        for layer in range(1, 6):
            soil_out[at, layer, :] = soil_mid[at, layer, :]


def local(
    soil_water,
    rainfall,
    drain_coef,
    cell_storage,
    release_rate,
    downstream,
    block_owner,
    outlet_reach,
    river_storage,
    river_lag,
):
    axes = ("tile", "grp")
    blocks = block_owner.shape[0]
    steps = blocks // CHUNK
    layers = soil_water.shape[0]

    def tiles(x):
        return x.reshape(layers, blocks, W).transpose(1, 0, 2)

    soil, coef = tiles(soil_water), tiles(drain_coef)
    rain, storage, rate, links = (
        x.reshape(blocks, W) for x in (rainfall, cell_storage, release_rate, downstream)
    )
    owner = block_owner.reshape(steps, CHUNK)
    reach = outlet_reach.reshape(steps, CHUNK)

    deep = pl.BlockSpec((CHUNK, layers, W), lambda i: (i, 0, 0))
    flat = pl.BlockSpec((CHUNK, W), lambda i: (i, 0))
    four = pl.BlockSpec((SUB, CHUNK, W), lambda i: (0, i, 0))

    def full(*shape):
        return pl.BlockSpec(shape, lambda i: (0,) * len(shape))

    f32 = jnp.float32
    shaped = jax.ShapeDtypeStruct
    params = pltpu.CompilerParams(vmem_limit_bytes=24 * MB)

    send = pl.pallas_call(
        moments_kernel,
        grid=(steps,),
        in_specs=[deep, deep, flat, flat, flat, flat, full(steps, CHUNK), full(steps, CHUNK)],
        out_specs=full(W, W),
        out_shape=shaped((W, W), f32),
        scratch_shapes=[pltpu.VMEM((CHUNK, W), f32), pltpu.VMEM((W, CHUNK), f32)],
        compiler_params=params,
        name="moments",
    )(soil, coef, rain, storage, rate, links, owner, reach)

    recv = lax.all_to_all(send, axes, split_axis=0, concat_axis=0, tiled=True)

    soil_mid, gains, hit, spot = pl.pallas_call(
        inflow_kernel,
        grid=(steps,),
        in_specs=[deep, deep, flat, flat, flat, flat, full(steps, CHUNK), full(steps, CHUNK)],
        out_specs=[deep, four, flat, flat],
        out_shape=[
            shaped((blocks, layers, W), f32),
            shaped((SUB, blocks, W), f32),
            shaped((blocks, W), jnp.bfloat16),
            shaped((blocks, W), jnp.int32),
        ],
        compiler_params=params,
        cost_estimate=pl.CostEstimate(flops=10_000_000, bytes_accessed=16 * MB, transcendentals=0),
        name="inflow",
    )(soil, coef, rain, storage, rate, links, owner, reach)

    fields = pl.pallas_call(
        reach_kernel,
        out_shape=shaped((W, FIELDS * W), f32),
        compiler_params=params,
        name="reaches",
    )(recv, river_storage, river_lag)

    fields = lax.all_to_all(fields, axes, split_axis=0, concat_axis=0, tiled=True)

    me = lax.axis_index(axes).astype(jnp.int32).reshape(1)
    soil_out, storage_out, section = pl.pallas_call(
        finish_kernel,
        grid=(steps,),
        in_specs=[
            pl.BlockSpec(memory_space=pltpu.SMEM),
            full(W, FIELDS * W),
            four,
            flat,
            flat,
            flat,
            flat,
            flat,
            deep,
        ],
        out_specs=[deep, flat, full(1, W)],
        out_shape=[
            shaped((blocks, layers, W), f32),
            shaped((blocks, W), f32),
            shaped((1, W), f32),
        ],
        scratch_shapes=[pltpu.VMEM((W, 3 * SUB * W), jnp.bfloat16), pltpu.VMEM((W, W), f32)],
        compiler_params=params,
        name="finish",
    )(me, fields, gains, storage, rate, links, hit, spot, soil_mid)

    soil_out = soil_out.transpose(1, 0, 2).reshape(layers, blocks * W)
    return (soil_out, storage_out.reshape(-1), section)


def solution(mesh):
    placed = (
        P(None, ("tile", "grp")),
        P(("tile", "grp")),
        P(None, ("tile", "grp")),
        P(("tile", "grp")),
        P(("tile", "grp")),
        P(("tile", "grp")),
        P(("tile", "grp"), None),
        P(("tile", "grp")),
        P("grp", "tile"),
        P("grp", "tile"),
    )
    return jax.shard_map(
        local,
        mesh=mesh,
        in_specs=placed,
        out_specs=(P(None, ("tile", "grp")), P(("tile", "grp")), P("grp", "tile")),
        check_vma=False,
    )
```

profile of v0, /device:TPU:1, one launch (start us, length us, event | category | flops | bytes accessed | tf_op | source)
XLA Modules:
  0.0 130.2 jit_solution(9661015877369971784)
XLA Ops:
  0.6 0.0 copy-start
  0.6 1.6 %copy-done = f32[6,65536]{1,0:T(8,128)S(1)} copy-done((f32[6,65536]{1,0:T(8,128)S(1)}, f32[6,65536]{1,0:T(8,128)}, u32[]{:S(2)}) %copy-start) | copy-done | bytes 1572888
  2.2 0.0 copy-start.2
  2.2 1.6 %copy-done.2 = f32[6,65536]{1,0:T(8,128)S(1)} copy-done((f32[6,65536]{1,0:T(8,128)S(1)}, f32[6,65536]{1,0:T(8,128)}, u32[]{:S(2)}) %copy-start.2) | copy-done | bytes 1572888
  3.8 0.0 copy-start.4
  3.8 0.9 copy-done.4
  4.8 0.0 copy-start.6
  4.8 0.9 copy-done.6
  5.7 0.0 copy-start.8
  5.7 0.9 copy-done.8
  6.7 0.0 copy-start.14
  6.7 0.9 copy-done.14
  7.6 0.0 copy-start.16
  7.6 0.7 copy-done.16
  8.3 0.0 copy-start.18
  8.3 0.7 copy-done.18
  9.0 0.0 copy-start.20
  9.0 0.0 copy-start.21
  9.0 6.7 %moments.1 = f32[128,128]{1,0:T(8,128)S(1)} custom-call(f32[512,6,128]{2,1,0:T(8,128)S(1)} %bitcast.25, f32[512,6,128]{2,1,0:T(8,128)S(1)} %bitcast.27, f32[512,128]{1,0:T(8,128)S(1)} %bitcast.40, f32[512,128]{1,0:T(8,128)S(1)} %bitcast.30, f32[512,128]{1,0:T(8,128)S(1)} %bitcast.33, s32[512,128]{1,0:T(8,128)S(1)} %bitcast.36, s32[4,128]{1,0:T(4,128)S(1)} %bitcast.44, ...), custom_call_target="tpu_custom_call" | custom-call | tf_op jit(solution)/shard_map/moments/pallas_call | solution.py:325
  15.6 0.0 copy-start.1
  15.7 0.0 copy-start.5
  15.7 0.0 copy-start.7
  15.7 0.0 copy-start.9
  15.7 0.0 copy-start.15
  15.7 0.0 copy-start.17
  15.7 0.0 copy-start.19
  15.7 21.2 %all_to_all.22 = f32[128,1,128]{2,1,0:T(1,128)S(1)} all-to-all(f32[128,1,128]{2,1,0:T(1,128)S(1)} %bitcast.42), channel_id=1, replica_groups=mesh['tile'=32,'grp'=4] {'tile','grp'}, dimensions={0} | all-to-all | bytes 131072 | tf_op jit(solution)/shard_map/all_to_all | solution.py:336
  36.9 0.0 copy-done.20
  36.9 0.0 copy-done.21
  37.0 0.5 reaches.1
  37.4 1.4 %copy.14 = f32[128,1,1152]{2,1,0:T(1,128)} copy(f32[128,1,1152]{2,0,1:T(8,128)S(1)} %bitcast.39) | data formatting | bytes 1179648 | tf_op jit(solution)/shard_map/all_to_all | solution.py:361
  38.9 4.8 %all-to-all-start.1 = ((f32[128,1,1152]{2,1,0:T(1,128)}), f32[128,1,1152]{2,1,0:T(1,128)}, u32[]{:S(2)}, u32[]{:S(2)}) async-start(f32[128,1,1152]{2,1,0:T(1,128)} %copy.14), calls=%async_computation.1 | async-start | bytes 1179648 | tf_op jit(solution)/shard_map/all_to_all | solution.py:361
  43.7 0.0 copy-done.1
  43.7 0.0 copy-done.5
  43.7 0.0 copy-done.7
  43.7 0.0 copy-done.9
  43.7 0.0 copy-done.15
  43.7 0.0 copy-done.17
  43.7 0.0 copy-done.19
  43.7 0.0 copy-start.3
  43.8 1.6 %copy-done.3 = f32[6,65536]{1,0:T(8,128)S(1)} copy-done((f32[6,65536]{1,0:T(8,128)S(1)}, f32[6,65536]{1,0:T(8,128)}, u32[]{:S(2)}) %copy-start.3) | copy-done | bytes 1572888
  45.3 72.9 %inflow.1 = (f32[512,6,128]{2,1,0:T(8,128)S(1)}, f32[4,512,128]{2,1,0:T(8,128)S(1)}, bf16[512,128]{1,0:T(8,128)(2,1)S(1)}, s32[512,128]{1,0:T(8,128)S(1)}) custom-call(f32[512,6,128]{2,1,0:T(8,128)S(1)} %bitcast.26, f32[512,6,128]{2,1,0:T(8,128)S(1)} %bitcast.28, f32[512,128]{1,0:T(8,128)S(1)} %bitcast.41, f32[512,128]{1,0:T(8,128)S(1)} %bitcast.31, ...), custom_call_target="tpu_custom_call" | custom-call | flops 10000000 | bytes 16777216 | tf_op jit(solution)/shard_map/inflow/pallas_call | solution.py:338
  118.2 0.0 copy-start.10
  118.2 1.3 %copy-done.10 = f32[512,6,128]{2,1,0:T(8,128)} copy-done((f32[512,6,128]{2,1,0:T(8,128)}, f32[512,6,128]{2,1,0:T(8,128)S(1)}, u32[]{:S(2)}) %copy-start.10) | copy-done | bytes 1572888
  119.5 0.0 copy-start.12
  119.5 1.0 copy-done.12
  120.5 0.0 all-to-all-done.1
  120.5 1.1 copy.17
  121.7 0.0 copy-start.11
  121.7 1.6 %copy-done.11 = f32[512,6,128]{2,1,0:T(8,128)S(1)} copy-done((f32[512,6,128]{2,1,0:T(8,128)S(1)}, f32[512,6,128]{2,1,0:T(8,128)}, u32[]{:S(2)}) %copy-start.11) | copy-done | bytes 1572888
  123.3 0.0 copy-start.13
  123.3 1.2 copy-done.13
  124.5 5.8 %finish.1 = (f32[512,6,128]{2,1,0:T(8,128)}, f32[512,128]{1,0:T(8,128)}, f32[1,128]{1,0:T(1,128)}) custom-call(s32[1]{0:T(128)} %bitcast.me, f32[128,1152]{1,0:T(8,128)S(1)} %bitcast.29, f32[4,512,128]{2,1,0:T(8,128)S(1)} %copy-done.13, f32[512,128]{1,0:T(8,128)S(1)} %bitcast.32, f32[512,128]{1,0:T(8,128)S(1)} %bitcast.35, s32[512,128]{1,0:T(8,128)S(1)} %bitcast.38, ...), custom_call_target="tpu_custom_call" | custom-call | tf_op jit(solution)/shard_map/finish/pallas_call | solution.py:364
Async XLA Ops:
  0.6 1.6 %copy-start = (f32[6,65536]{1,0:T(8,128)S(1)}, f32[6,65536]{1,0:T(8,128)}, u32[]{:S(2)}) copy-start(f32[6,65536]{1,0:T(8,128)} %param.10) | copy-start | bytes 4718596
  2.2 1.6 %copy-start.2 = (f32[6,65536]{1,0:T(8,128)S(1)}, f32[6,65536]{1,0:T(8,128)}, u32[]{:S(2)}) copy-start(f32[6,65536]{1,0:T(8,128)} %param.12) | copy-start | bytes 4718596
  3.8 0.9 copy-start.4
  4.8 0.9 copy-start.6
  5.7 0.9 copy-start.8
  6.7 0.9 copy-start.14
  7.6 0.7 copy-start.16
  8.3 0.7 copy-start.18
  9.0 28.0 %copy-start.20 = (f32[1,128]{1,0:T(1,128)S(1)}, f32[1,128]{1,0:T(1,128)}, u32[]{:S(2)}) copy-start(f32[1,128]{1,0:T(1,128)} %volume.1) | copy-start | bytes 1540
  9.0 28.0 %copy-start.21 = (f32[1,128]{1,0:T(1,128)S(1)}, f32[1,128]{1,0:T(1,128)}, u32[]{:S(2)}) copy-start(f32[1,128]{1,0:T(1,128)} %lag.1) | copy-start | bytes 1540
  15.6 28.0 %copy-start.1 = (f32[6,65536]{1,0:T(8,128)S(1)}, f32[6,65536]{1,0:T(8,128)}, u32[]{:S(2)}) copy-start(f32[6,65536]{1,0:T(8,128)} %param.10) | copy-start | bytes 4718596
  15.7 28.0 %copy-start.5 = (f32[65536]{0:T(1024)S(1)}, f32[65536]{0:T(1024)}, u32[]{:S(2)}) copy-start(f32[65536]{0:T(1024)} %param.13) | copy-start | bytes 786436
  15.7 28.0 %copy-start.7 = (f32[65536]{0:T(1024)S(1)}, f32[65536]{0:T(1024)}, u32[]{:S(2)}) copy-start(f32[65536]{0:T(1024)} %param.14) | copy-start | bytes 786436
  15.7 28.0 %copy-start.9 = (s32[65536]{0:T(1024)S(1)}, s32[65536]{0:T(1024)}, u32[]{:S(2)}) copy-start(s32[65536]{0:T(1024)} %param.15) | copy-start | bytes 786436
  15.7 28.0 %copy-start.15 = (f32[65536]{0:T(1024)S(1)}, f32[65536]{0:T(1024)}, u32[]{:S(2)}) copy-start(f32[65536]{0:T(1024)} %param.11) | copy-start | bytes 786436
  15.7 28.0 %copy-start.17 = (s32[512,1]{0,1:T(1,128)S(1)}, s32[512,1]{0,1:T(1,128)}, u32[]{:S(2)}) copy-start(s32[512,1]{0,1:T(1,128)} %param.16) | copy-start | bytes 6148
  15.7 28.0 %copy-start.19 = (s32[512]{0:T(512)S(1)}, s32[512]{0:T(512)}, u32[]{:S(2)}) copy-start(s32[512]{0:T(512)} %param.17) | copy-start | bytes 6148
  38.9 81.7 %all-to-all-start.1 = ((f32[128,1,1152]{2,1,0:T(1,128)}), f32[128,1,1152]{2,1,0:T(1,128)}, u32[]{:S(2)}, u32[]{:S(2)}) async-start(f32[128,1,1152]{2,1,0:T(1,128)} %copy.14), calls=%async_computation.1 | async-start | bytes 1179648 | tf_op jit(solution)/shard_map/all_to_all | solution.py:361
  43.7 1.6 %copy-start.3 = (f32[6,65536]{1,0:T(8,128)S(1)}, f32[6,65536]{1,0:T(8,128)}, u32[]{:S(2)}) copy-start(f32[6,65536]{1,0:T(8,128)} %param.12) | copy-start | bytes 4718596
  118.2 1.3 %copy-start.10 = (f32[512,6,128]{2,1,0:T(8,128)}, f32[512,6,128]{2,1,0:T(8,128)S(1)}, u32[]{:S(2)}) copy-start(f32[512,6,128]{2,1,0:T(8,128)S(1)} %get-tuple-element.13.soil_mid) | copy-start | bytes 4718596
  119.5 1.0 copy-start.12
  121.7 1.6 %copy-start.11 = (f32[512,6,128]{2,1,0:T(8,128)S(1)}, f32[512,6,128]{2,1,0:T(8,128)}, u32[]{:S(2)}) copy-start(f32[512,6,128]{2,1,0:T(8,128)} %copy-done.10) | copy-start | bytes 4718596
  123.3 1.2 copy-start.13
where the time goes:
time: 131 us; the launch traced here: 130 us
  Pallas kernels  85.8 us (65%)
  blocking collectives  21.2 us (16%)
  local copies, waits for them, and re-layouts  17.6 us (13%)
  starting transfers between devices  4.79 us (4%)
    pallas_call x1, Pallas kernels, local(): pl.pallas_call(inflow_kernel, grid=(steps,), in_specs=[deep, deep, flat,...  72.9 us
    all_to_all x1, blocking collectives, local(): recv = lax.all_to_all(send, axes, split_axis=0, concat_axis=0, tiled=True)  21.2 us
    unnamed x45, local copies, waits for them, and re-layouts  16.2 us
    pallas_call x1, Pallas kernels, local(): pl.pallas_call(moments_kernel, grid=(steps,), in_specs=[deep, deep, flat,...  6.65 us
    pallas_call x1, Pallas kernels, local(): pl.pallas_call(finish_kernel, grid=(steps,), in_specs=[pl.BlockSpec(memor...  5.76 us
    all_to_all x1, starting transfers between devices, local(): lax.all_to_all(fields, axes, split_axis=0, concat_axis=0, tiled=True)  4.79 us
  transfers between devices with their start and end apart: 1, of which 0 were waited for; matrix products, arithmetic and copies ran while one was open for 0% of the time, Pallas kernels for 56%

commit v1 on v0

v1 whole, which is shorter than its diff:
```python
import jax
import jax.numpy as jnp
from jax import lax
from jax.experimental import pallas as pl
from jax.experimental.pallas import tpu as pltpu
from jax.sharding import PartitionSpec as P

SUB = 4
recharge_share = 0.2

W = 128
CHUNK = 128
PARTS = 2
FIELDS = 9
MB = 1024 * 1024


def gat(values, index):
    return jnp.take_along_axis(values, index, axis=1, mode="promise_in_bounds")


def iota(shape, dim):
    return lax.broadcasted_iota(jnp.int32, shape, dim)


def split3(x):
    hi = x.astype(jnp.bfloat16)
    rest = x - hi.astype(jnp.float32)
    mid = rest.astype(jnp.bfloat16)
    low = (rest - mid.astype(jnp.float32)).astype(jnp.bfloat16)
    return hi, mid, low


def pick(onehot, x):
    hi, mid, low = split3(x)
    dot = lambda part: jnp.dot(onehot, part, preferred_element_type=jnp.float32)
    return dot(hi) + dot(mid) + dot(low)


def run_all(copies):
    for copy in copies:
        copy.start()
    return copies


def wait_all(copies):
    for copy in copies:
        copy.wait()


def moments_kernel(
    soil, coef, rain, storage, rate, links, owner, reach, send, top, low, low_coef, rain_v, s_v, r_v, to_v, pack_v, sems
):
    lane = iota((W, W), 1)
    sub = iota((W, W), 0)
    steps = owner.shape[0]
    rows = s_v.shape[0] // PARTS
    loads = []
    for part in range(PARTS):
        at = pl.ds(part * rows, rows)
        pairs = (
            (links.at[at], to_v.at[at]),
            (rate.at[at], r_v.at[at]),
            (storage.at[at], s_v.at[at]),
            (rain.at[at], rain_v.at[at]),
            (soil.at[at, 0, :], top.at[at]),
            (soil.at[at, 5, :], low.at[at]),
            (coef.at[at, 5, :], low_coef.at[at]),
        )
        loads.append(
            run_all(
                [
                    pltpu.make_async_copy(src, dst, sems.at[part, k])
                    for k, (src, dst) in enumerate(pairs)
                ]
            )
        )

    before = (sub < lane).astype(jnp.bfloat16)
    hits = []
    carry = jnp.zeros((W, 1), jnp.float32)
    for step in range(steps):
        own = jnp.broadcast_to(owner[step : step + 1, :], (W, CHUNK))
        hit = (own == sub).astype(jnp.float32)
        hit16 = hit.astype(jnp.bfloat16)
        hits.append(hit16)
        seen = jnp.dot(hit16, before, preferred_element_type=jnp.float32) + carry
        carry = carry + jnp.sum(hit, axis=1, keepdims=True)
        rank = jnp.sum(hit * seen, axis=0, keepdims=True)
        both = rank + 8.0 * reach[step : step + 1, :].astype(jnp.float32)
        both = jnp.transpose(jnp.broadcast_to(both, (W, CHUNK)))
        pack_v[step * CHUNK : (step + 1) * CHUNK, :] = both

    for part in range(PARTS):
        at = slice(part * rows, (part + 1) * rows)
        wait_all(loads[part])
        w0, w5 = top[at, :], low[at, :]
        s, r, down = s_v[at, :], r_v[at, :], to_v[at, :]
        share = (rain_v[at, :] * w0 * w0 + low_coef[at, :] * w5 * w5 * w5) * (1.0 / SUB)
        leaves = down == W
        to = down & (W - 1)
        follow = lambda v: jnp.where(leaves, 0.0, gat(v, to))
        a1 = jnp.where(leaves, r, 0.0)
        a2 = a1 * r
        a3 = a2 * r
        g = follow(a1)
        w_1 = r * g
        w_2 = w_1 * g
        w_3 = w_2 * g
        x_1 = r * follow(w_1)
        x_2 = r * follow(w_2)
        z = w_1 * (1.0 - r) + x_1
        y = r * follow(z)
        e1 = (1.0 - r) * s + share
        h1 = a1 * share
        h2 = a2 * share
        terms = (
            a1 * s,
            a2 * s,
            a3 * s,
            a3 * r * s,
            h1 + w_1 * s,
            h2 + w_2 * s,
            a3 * share + w_3 * s,
            h1 + w_1 * e1 + x_1 * s,
            h2 + w_2 * e1 + x_2 * s,
            h1 + w_1 * share + z * e1 + y * s,
        )
        lane_p = iota((rows, W), 1)
        field = lane_p & 15
        both = pack_v[at, :].astype(jnp.int32)
        out = (both >> 3).astype(jnp.float32)
        for f, term in enumerate(terms):
            out = jnp.where(field == f, jnp.sum(term, axis=1, keepdims=True), out)
        pack_v[at, :] = jnp.where((lane_p >> 4) == (both & 7), out, 0.0)

    total = jnp.zeros((W, W), jnp.float32)
    for step in range(steps):
        total = total + pick(hits[step], pack_v[step * CHUNK : (step + 1) * CHUNK, :])
    send[...] = total


def soil_kernel(soil, coef, rain, after, owner, reach, soil_mid, mid0, share, hit, spot, water_v, coef_v, out_v, rain_v, sems, out_sems):
    del after
    layers = water_v.shape[0]
    loads = run_all([pltpu.make_async_copy(rain, rain_v, sems.at[0, layers])])
    for layer in range(layers):
        loads.append(pltpu.make_async_copy(soil.at[:, layer, :], water_v.at[layer], sems.at[0, layer]))
        loads.append(pltpu.make_async_copy(coef.at[:, layer, :], coef_v.at[layer], sems.at[1, layer]))
    run_all(loads[1:])
    sub = iota((W, W), 0)
    for step in range(owner.shape[0]):
        at = slice(step * CHUNK, (step + 1) * CHUNK)
        own = jnp.broadcast_to(owner[step : step + 1, :], (W, CHUNK))
        hit[at, :] = jnp.transpose((own == sub).astype(jnp.float32)).astype(jnp.bfloat16)
        place = jnp.broadcast_to(reach[step : step + 1, :].astype(jnp.float32), (W, CHUNK))
        spot[at, :] = jnp.transpose(place).astype(jnp.int32)
    loads[0].wait()
    stores = []
    coming = surface = None
    for layer in range(layers):
        wait_all(loads[1 + 2 * layer : 3 + 2 * layer])
        water = water_v[layer]
        if layer == 0:
            surface = rain_v[...] * water * water
            coming = rain_v[...] - surface
        drained = coef_v[layer] * water * water * water
        mid = water + coming - drained
        coming = drained
        if layer == 0:
            mid0[...] = mid
        else:
            out_v[layer] = mid
            copy = pltpu.make_async_copy(out_v.at[layer], soil_mid.at[:, layer, :], out_sems.at[layer])
            copy.start()
            stores.append(copy)
    share[...] = (surface + coming) * (1.0 / SUB)
    wait_all(stores)


def inflow_kernel(share, storage, rate, links, gains, key_v, s_v):
    shape = share.shape
    lane = iota(shape, 1)
    key_v[...] = (links[...] * W + lane).astype(jnp.float32)
    size = 2
    while size <= W:
        j = size // 2
        while j >= 1:
            key = key_v[...]
            other = gat(key, lane ^ j)
            low = ((lane & j) == 0) == ((lane & size) == 0)
            key_v[...] = jnp.where(low, jnp.minimum(key, other), jnp.maximum(key, other))
            j //= 2
        size *= 2
    key = key_v[...].astype(jnp.int32)
    order = key & (W - 1)
    dest = key >> 7
    count = jnp.zeros(shape, jnp.int32)
    for shift in (64, 32, 16, 8, 4, 2, 1):
        nxt = count + shift
        count = jnp.where(gat(dest, nxt - 1) <= lane, nxt, count)
    earlier = jnp.where(lane == 0, 0, pltpu.roll(count, 1, 1))
    ahead = (iota((W, W), 0) < iota((W, W), 1)).astype(jnp.bfloat16)
    s_v[...] = storage[...]
    for n in range(SUB):
        s = s_v[...]
        release = rate[...] * s
        run = jnp.zeros(shape, jnp.float32)
        for part in split3(gat(release, order)):
            run = run + jnp.dot(part, ahead, preferred_element_type=jnp.float32)
        gain = share[...] + (gat(run, count) - gat(run, earlier))
        gains[n] = gain
        s_v[...] = s + gain - release


def reach_kernel(recv, volume, lag, out):
    got = recv[...]
    turned = jnp.transpose(got)
    lane = iota((W, W), 1)
    total = jnp.zeros((48, W), jnp.float32)
    for c in range(8):
        at = jnp.broadcast_to(got[:, c * 16 + 10 : c * 16 + 11], (W, W)).astype(jnp.int32)
        hit = (at == lane).astype(jnp.bfloat16)
        parts = jnp.concatenate(split3(turned[c * 16 : c * 16 + 16, :]), axis=0)
        total += jnp.dot(parts, hit, preferred_element_type=jnp.float32)
    total = total[:16, :] + total[16:32, :] + total[32:, :]
    row = lambda f: total[f : f + 1, :]
    vol = volume[...]
    back = 1.0 / (1.0 + vol)
    lateral = back * row(0) * (1.0 / W)
    s1 = row(0) - back * row(1) + row(4)
    s2 = row(1) - back * row(2) + row(5)
    s3 = row(2) - back * row(3) + row(6)
    fields = (lag[...], vol, lateral, s1, s2, s3, row(7), row(8), row(9))
    wide = [jnp.broadcast_to(value, (8, W)) for value in fields]
    sub = iota((8, W), 0)
    period = []
    for k in range(FIELDS):
        tile = jnp.zeros((8, W), jnp.float32)
        for i in range(8):
            tile = jnp.where(sub == i, wide[(k * 8 + i) % FIELDS], tile)
        period.append(tile)
    for k in range(W // 8):
        for f in range(FIELDS):
            at = (k * FIELDS + f) * 8
            out[at : at + 8, :] = period[f]


def shift_rows(x, by, fill):
    return jnp.concatenate([jnp.full((by, W), fill, x.dtype), x[:-by, :]], axis=0)


def finish_kernel(
    me, fields, gains, storage, rate, links, hit, spot, mid0, soil_mid, soil_out, storage_out, section,
    table, flow_ref, g_v, s_v, r_v, to_v, hit_v, spot_v, mid_v, out_v, top_v, sems, out_sems
):
    del soil_mid
    lane = iota((W, W), 1)
    loads = run_all(
        [
            pltpu.make_async_copy(src, dst, sems.at[k])
            for k, (src, dst) in enumerate(
                (
                    (hit, hit_v),
                    (spot, spot_v),
                    (storage, s_v),
                    (rate, r_v),
                    (links, to_v),
                    (gains, g_v),
                    (mid0, mid_v),
                )
            )
        ]
    )
    field = lambda f: fields[pl.ds(f, W, FIELDS), :]
    lag = field(0)
    weight = 1.0 / (1.0 + lag)
    stages = []
    base = weight
    total = weight
    stride = 1
    for radix in (4, 4, 8):
        neutral = total
        gains_of = []
        product = base
        for d in range(1, radix):
            ok = lane >= d * stride
            gains_of.append((d * stride, jnp.where(ok, product, 0.0)))
            product = product * pltpu.roll(base, d * stride, 1)
            neutral = neutral * jnp.where(ok, pltpu.roll(total, d * stride, 1), 1.0)
        stages.append(gains_of)
        base, total = product, neutral
        stride *= radix
    last = jnp.broadcast_to(total[:, W - 1 : W], (W, W))
    hops = []
    jump = last
    by = 4
    while by < W:
        hops.append((by, jump))
        jump = jump * shift_rows(jump, by, 0.0)
        by *= 2

    volume = field(1)
    lateral = field(2)
    s1, s2, s3 = field(3), field(4), field(5)
    c11, c12, c21 = field(6), field(7), field(8)
    flow = volume
    for n in range(SUB):
        back = 1.0 / (1.0 + volume)
        for part, value in enumerate(split3(back)):
            table[:, (part * SUB + n) * W : (part * SUB + n + 1) * W] = value
        if n == 1:
            lateral = back * s1 * (1.0 / W)
            s1, s2 = s1 - back * s2 + c11, s2 - back * s3 + c12
        elif n == 2:
            lateral = back * s1 * (1.0 / W)
            s1 = s1 - back * s2 + c21
        elif n == 3:
            lateral = back * s1 * (1.0 / W)
        run = weight * (volume + lateral)
        for gains_of in stages:
            add = run
            for d, gain in gains_of:
                add = add + gain * pltpu.roll(run, d, 1)
            run = add
        head = jnp.broadcast_to(run[:, W - 1 : W], (W, W))
        for by, jump in hops:
            head = head + jump * shift_rows(head, by, 0.0)
        flow = run + total * shift_rows(head, 4, 0.0)
        volume = lag * flow
    flow_ref[...] = flow
    section[...] = jnp.log1p(flow_ref[pl.ds(me[0], 1), :])

    wait_all(loads)
    stores = []
    blocks = s_v.shape[0]
    for step in range(blocks // CHUNK):
        at = slice(step * CHUNK, (step + 1) * CHUNK)
        got = jnp.dot(hit_v[at, :], table[...], preferred_element_type=jnp.float32)
        place = spot_v[at, :]
        s, r = s_v[at, :], r_v[at, :]
        leaves = to_v[at, :] == W
        for n in range(SUB):
            part = lambda k: got[:, (k * SUB + n) * W : (k * SUB + n + 1) * W]
            back = gat(part(0) + part(1) + part(2), place)
            s = s - r * jnp.where(leaves, back, 1.0) * s + g_v[n, at, :]
        out_v[at, :] = s
        top = mid_v[at, :]
        top_v[at, :] = top + recharge_share * (s / (s + 1.0)) * (1.0 - top)
        where = pl.ds(step * CHUNK, CHUNK)
        stores += run_all(
            [
                pltpu.make_async_copy(out_v.at[where], storage_out.at[where], out_sems.at[0, step]),
                pltpu.make_async_copy(top_v.at[where], soil_out.at[where, 0, :], out_sems.at[1, step]),
            ]
        )
    wait_all(stores)


def local(
    soil_water,
    rainfall,
    drain_coef,
    cell_storage,
    release_rate,
    downstream,
    block_owner,
    outlet_reach,
    river_storage,
    river_lag,
):
    axes = ("tile", "grp")
    blocks = block_owner.shape[0]
    steps = blocks // CHUNK
    layers = soil_water.shape[0]

    def tiles(x):
        return x.reshape(layers, blocks, W).transpose(1, 0, 2)

    soil, coef = tiles(soil_water), tiles(drain_coef)
    rain, storage, rate, links = (
        x.reshape(blocks, W) for x in (rainfall, cell_storage, release_rate, downstream)
    )
    owner = block_owner.reshape(steps, CHUNK)
    reach = outlet_reach.reshape(steps, CHUNK)

    f32 = jnp.float32
    i32 = jnp.int32
    b16 = jnp.bfloat16
    shaped = jax.ShapeDtypeStruct
    vmem = pl.BlockSpec(memory_space=pltpu.VMEM)
    hbm = pl.BlockSpec(memory_space=pltpu.HBM)
    params = pltpu.CompilerParams(vmem_limit_bytes=24 * MB)
    alone = pltpu.CompilerParams(vmem_limit_bytes=60 * MB)
    scratch = lambda dtype, *shape: pltpu.VMEM(shape, dtype)
    flat = lambda dtype: scratch(dtype, blocks, W)
    sems = lambda *shape: pltpu.SemaphoreType.DMA(shape)
    cost = lambda flops, moved: pl.CostEstimate(flops=flops, bytes_accessed=moved, transcendentals=0)

    send = pl.pallas_call(
        moments_kernel,
        in_specs=[hbm] * 6 + [vmem] * 2,
        out_specs=vmem,
        out_shape=shaped((W, W), f32),
        scratch_shapes=[flat(f32)] * 6 + [flat(i32), flat(f32), sems(PARTS, 7)],
        compiler_params=alone,
        name="moments",
    )(soil, coef, rain, storage, rate, links, owner, reach)

    recv = lax.all_to_all(send, axes, split_axis=0, concat_axis=0, tiled=True)

    soil_mid, mid0, share, hit, spot = pl.pallas_call(
        soil_kernel,
        in_specs=[hbm] * 4 + [vmem] * 2,
        out_specs=[hbm] + [vmem] * 4,
        out_shape=[
            shaped((blocks, layers, W), f32),
            shaped((blocks, W), f32),
            shaped((blocks, W), f32),
            shaped((blocks, W), b16),
            shaped((blocks, W), i32),
        ],
        scratch_shapes=[scratch(f32, layers, blocks, W)] * 3 + [flat(f32), sems(2, layers + 1), sems(layers)],
        compiler_params=alone,
        cost_estimate=cost(3_000_000, 10 * MB),
        name="soil",
    )(soil, coef, rain, send, owner, reach)

    recv, share = lax.optimization_barrier((recv, share))

    gains = pl.pallas_call(
        inflow_kernel,
        in_specs=[vmem] * 4,
        out_specs=vmem,
        out_shape=shaped((SUB, blocks, W), f32),
        scratch_shapes=[flat(f32)] * 2,
        compiler_params=params,
        cost_estimate=cost(10_000_000, 16 * MB),
        name="inflow",
    )(share, storage, rate, links)

    fields = pl.pallas_call(
        reach_kernel,
        in_specs=[vmem] * 3,
        out_specs=vmem,
        out_shape=shaped((W * FIELDS, W), f32),
        compiler_params=params,
        name="reaches",
    )(recv, river_storage, river_lag)

    fields = fields.reshape(W, 1, FIELDS * W)
    fields = lax.all_to_all(fields, axes, split_axis=0, concat_axis=0, tiled=True)
    fields = fields.reshape(W * FIELDS, W)

    me = lax.axis_index(axes).astype(jnp.int32).reshape(1)
    soil_out, storage_out, section = pl.pallas_call(
        finish_kernel,
        in_specs=[pl.BlockSpec(memory_space=pltpu.SMEM), vmem] + [hbm] * 8,
        out_specs=[hbm, hbm, vmem],
        out_shape=[
            shaped((blocks, layers, W), f32),
            shaped((blocks, W), f32),
            shaped((1, W), f32),
        ],
        scratch_shapes=[
            scratch(b16, W, 3 * SUB * W),
            scratch(f32, W, W),
            scratch(f32, SUB, blocks, W),
            flat(f32),
            flat(f32),
            flat(i32),
            flat(b16),
            flat(i32),
            flat(f32),
            flat(f32),
            flat(f32),
            sems(7),
            sems(2, steps),
        ],
        input_output_aliases={9: 0},
        compiler_params=params,
        name="finish",
    )(me, fields, gains, storage, rate, links, hit, spot, mid0, soil_mid)

    soil_out = soil_out.transpose(1, 0, 2).reshape(layers, blocks * W)
    return (soil_out, storage_out.reshape(-1), section)


def solution(mesh):
    placed = (
        P(None, ("tile", "grp")),
        P(("tile", "grp")),
        P(None, ("tile", "grp")),
        P(("tile", "grp")),
        P(("tile", "grp")),
        P(("tile", "grp")),
        P(("tile", "grp"), None),
        P(("tile", "grp")),
        P("grp", "tile"),
        P("grp", "tile"),
    )
    return jax.shard_map(
        local,
        mesh=mesh,
        in_specs=placed,
        out_specs=(P(None, ("tile", "grp")), P(("tile", "grp")), P("grp", "tile")),
        check_vma=False,
    )
```

time: 131 us -> 52.6 us (0.40)
  Pallas kernels: 85.8 us -> 21.7 us
  blocking collectives: 21.2 us -> 0 us
  local copies, waits for them, and re-layouts: 17.6 us -> 0.99 us
  waiting for transfers between devices: 0.01 us -> 12.7 us
  starting transfers between devices: 4.79 us -> 16 us
    pallas_call x4 -> x5, Pallas kernels: 85.8 us -> 21.7 us  [the longest x1 6.42 us: local(): pl.pallas_call(inflow_kernel, in_specs=[vmem] * 4, out_specs=vmem, out_sh...]
    all_to_all x1 -> x0, blocking collectives: 21.2 us -> none  [local(): recv = lax.all_to_all(send, axes, split_axis=0, concat_axis=0, tiled=True)]
    unnamed x45 -> x18, local copies, waits for them, and re-layouts: 16.2 us -> 0.99 us
    all_to_all x0 -> x1, starting transfers between devices: none -> 11.5 us  [local(): recv = lax.all_to_all(send, axes, split_axis=0, concat_axis=0, tiled=True)]
    all_to_all x1, waiting for transfers between devices: 0.01 us -> 7.39 us  [local(): lax.all_to_all(fields, axes, split_axis=0, concat_axis=0, tiled=True)]
    all_to_all x0 -> x1, waiting for transfers between devices: none -> 5.31 us  [local(): recv = lax.all_to_all(send, axes, split_axis=0, concat_axis=0, tiled=True)]
    all_to_all x1 -> x0, local copies, waits for them, and re-layouts: 1.42 us -> none  [local(): lax.all_to_all(fields, axes, split_axis=0, concat_axis=0, tiled=True)]
  transfers between devices with their start and end apart: 1 -> 2, of which waited for: 0 -> 2; matrix products, arithmetic and copies ran while one was open for 0% -> 0% of each run, Pallas kernels for 56% -> 21%
where the time goes in v1:
time: 52.6 us; the launch traced here: 52.3 us
  Pallas kernels  21.7 us (41%)
  starting transfers between devices  16 us (30%)
  waiting for transfers between devices  12.7 us (24%)
  local copies, waits for them, and re-layouts  0.99 us (2%)
  between operations  0.93 us (2%)
    all_to_all x1, starting transfers between devices, local(): recv = lax.all_to_all(send, axes, split_axis=0, concat_axis=0, tiled=True)  11.5 us
    all_to_all x1, waiting for transfers between devices, local(): lax.all_to_all(fields, axes, split_axis=0, concat_axis=0, tiled=True)  7.39 us
    pallas_call x1, Pallas kernels, local(): pl.pallas_call(inflow_kernel, in_specs=[vmem] * 4, out_specs=vmem, out_sh...  6.42 us
    all_to_all x1, waiting for transfers between devices, local(): recv = lax.all_to_all(send, axes, split_axis=0, concat_axis=0, tiled=True)  5.31 us
    pallas_call x1, Pallas kernels, local(): pl.pallas_call(finish_kernel, in_specs=[pl.BlockSpec(memory_space=pltpu.S...  4.99 us
    pallas_call x1, Pallas kernels, local(): pl.pallas_call(soil_kernel, in_specs=[hbm] * 4 + [vmem] * 2, out_specs=[h...  4.51 us
    pallas_call x1, Pallas kernels, local(): pl.pallas_call(moments_kernel, in_specs=[hbm] * 6 + [vmem] * 2, out_specs...  4.49 us
    all_to_all x1, starting transfers between devices, local(): lax.all_to_all(fields, axes, split_axis=0, concat_axis=0, tiled=True)  4.48 us
  transfers between devices with their start and end apart: 2, of which 2 were waited for; matrix products, arithmetic and copies ran while one was open for 0% of the time, Pallas kernels for 21%

profile of v1, /device:TPU:1, one launch (start us, length us, event | category | flops | bytes accessed | tf_op | source)
XLA Modules:
  0.0 52.3 jit_solution(14678044340315386679)
XLA Ops:
  0.6 4.5 %moments.1.after = f32[128,128]{1,0:T(8,128)} custom-call(f32[512,6,128]{2,1,0:T(8,128)} %bitcast.34, f32[512,6,128]{2,1,0:T(8,128)} %bitcast.36, f32[512,128]{1,0:T(8,128)} %bitcast.39, f32[512,128]{1,0:T(8,128)} %bitcast.24, f32[512,128]{1,0:T(8,128)} %bitcast.27, s32[512,128]{1,0:T(8,128)} %bitcast.30, s32[4,128]{1,0:T(4,128)} %bitcast.42, s32[4,128]{1,0:T(4,128)} %bitcast.44), custom_call_target="tpu_custom_call" | custom-call | tf_op jit(solution)/shard_map/moments/pallas_call | solution.py:400
  5.1 11.5 %all-to-all-start = ((f32[128,1,128]{2,1,0:T(1,128)}), f32[128,1,128]{2,1,0:T(1,128)S(1)}, u32[]{:S(2)}, u32[]{:S(2)}) async-start(f32[128,1,128]{2,1,0:T(1,128)} %bitcast.41), calls=%async_computation | async-start | bytes 131072 | tf_op jit(solution)/shard_map/all_to_all | solution.py:410
  16.6 0.0 copy-start.7
  16.6 0.0 copy-start.8
  16.6 0.0 copy-start
  16.7 0.0 copy-start.1
  16.7 0.0 copy-start.2
  16.7 4.5 %soil.1 = (f32[512,6,128]{2,1,0:T(8,128)}, f32[512,128]{1,0:T(8,128)}, f32[512,128]{1,0:T(8,128)}, bf16[512,128]{1,0:T(8,128)(2,1)}, s32[512,128]{1,0:T(8,128)}) custom-call(f32[512,6,128]{2,1,0:T(8,128)} %bitcast.35, f32[512,6,128]{2,1,0:T(8,128)} %bitcast.37, f32[512,128]{1,0:T(8,128)} %bitcast.40, f32[128,128]{1,0:T(8,128)} %moments.1.after, ...), custom_call_target="tpu_custom_call" | custom-call | flops 3000000 | bytes 10485760 | tf_op jit(solution)/shard_map/soil/pallas_call | solution.py:412
  21.2 0.0 copy-start.4
  21.2 0.0 copy-start.5
  21.2 0.0 copy-start.6
  21.2 5.3 %all-to-all-done = f32[128,1,128]{2,1,0:T(1,128)S(1)} async-done(((f32[128,1,128]{2,1,0:T(1,128)}), f32[128,1,128]{2,1,0:T(1,128)S(1)}, u32[]{:S(2)}, u32[]{:S(2)}) %all-to-all-start) | async-done | bytes 65568 | tf_op jit(solution)/shard_map/all_to_all | solution.py:410
  26.5 0.0 copy-done.7
  26.5 0.0 copy-done.8
  26.5 1.3 %reaches.1 = f32[1152,128]{1,0:T(8,128)} custom-call(f32[128,128]{1,0:T(8,128)S(1)} %bitcast.33, f32[1,128]{1,0:T(1,128)S(1)} %copy-done.7, f32[1,128]{1,0:T(1,128)S(1)} %copy-done.8), custom_call_target="tpu_custom_call" | custom-call | tf_op jit(solution)/shard_map/reaches/pallas_call | solution.py:442
  27.9 4.5 %all-to-all-start.1 = ((f32[128,1,1152]{2,1,0:T(1,128)}), f32[128,1,1152]{2,1,0:T(1,128)S(1)}, u32[]{:S(2)}, u32[]{:S(2)}) async-start(f32[128,1,1152]{2,1,0:T(1,128)} %bitcast.16), calls=%async_computation.1 | async-start | bytes 1179648 | tf_op jit(solution)/shard_map/all_to_all | solution.py:452
  32.4 0.0 copy-done
  32.4 0.0 copy-done.1
  32.4 0.0 copy-done.2
  32.4 0.0 copy-start.3
  32.4 0.9 %copy-done.3 = f32[512,128]{1,0:T(8,128)S(1)} copy-done((f32[512,128]{1,0:T(8,128)S(1)}, f32[512,128]{1,0:T(8,128)}, u32[]{:S(2)}) %copy-start.3) | copy-done | bytes 262168
  33.3 6.4 %inflow.1.gains = f32[4,512,128]{2,1,0:T(8,128)S(1)} custom-call(f32[512,128]{1,0:T(8,128)S(1)} %copy-done.3, f32[512,128]{1,0:T(8,128)S(1)} %bitcast.25, f32[512,128]{1,0:T(8,128)S(1)} %bitcast.28, s32[512,128]{1,0:T(8,128)S(1)} %bitcast.31), custom_call_target="tpu_custom_call" | custom-call | flops 10000000 | bytes 16777216 | tf_op jit(solution)/shard_map/inflow/pallas_call | solution.py:431
  39.8 7.4 %all-to-all-done.1 = f32[128,1,1152]{2,1,0:T(1,128)S(1)} async-done(((f32[128,1,1152]{2,1,0:T(1,128)}), f32[128,1,1152]{2,1,0:T(1,128)S(1)}, u32[]{:S(2)}, u32[]{:S(2)}) %all-to-all-start.1) | async-done | bytes 589856 | tf_op jit(solution)/shard_map/all_to_all | solution.py:452
  47.1 0.0 copy-done.4
  47.2 0.0 copy-done.5
  47.2 0.0 copy-done.6
  47.2 5.0 %finish.1 = (f32[512,6,128]{2,1,0:T(8,128)}, f32[512,128]{1,0:T(8,128)}, f32[1,128]{1,0:T(1,128)}) custom-call(s32[1]{0:T(128)} %bitcast.me, f32[1152,128]{1,0:T(8,128)S(1)} %bitcast.23, f32[4,512,128]{2,1,0:T(8,128)S(1)} %inflow.1.gains, f32[512,128]{1,0:T(8,128)S(1)} %bitcast.26, f32[512,128]{1,0:T(8,128)S(1)} %bitcast.29, ...), custom_call_target="tpu_custom_call", output_to_operand_aliasing={{0}: (9, {})} | custom-call | tf_op jit(solution)/shard_map/finish/pallas_call | solution.py:456
Async XLA Ops:
  5.1 21.4 %all-to-all-start = ((f32[128,1,128]{2,1,0:T(1,128)}), f32[128,1,128]{2,1,0:T(1,128)S(1)}, u32[]{:S(2)}, u32[]{:S(2)}) async-start(f32[128,1,128]{2,1,0:T(1,128)} %bitcast.41), calls=%async_computation | async-start | bytes 131072 | tf_op jit(solution)/shard_map/all_to_all | solution.py:410
  16.6 9.9 %copy-start.7 = (f32[1,128]{1,0:T(1,128)S(1)}, f32[1,128]{1,0:T(1,128)}, u32[]{:S(2)}) copy-start(f32[1,128]{1,0:T(1,128)} %volume.1) | copy-start | bytes 1540
  16.6 9.9 %copy-start.8 = (f32[1,128]{1,0:T(1,128)S(1)}, f32[1,128]{1,0:T(1,128)}, u32[]{:S(2)}) copy-start(f32[1,128]{1,0:T(1,128)} %lag.1) | copy-start | bytes 1540
  16.6 15.7 %copy-start = (f32[65536]{0:T(1024)S(1)}, f32[65536]{0:T(1024)}, u32[]{:S(2)}) copy-start(f32[65536]{0:T(1024)} %param.13) | copy-start | bytes 786436
  16.7 15.7 %copy-start.1 = (f32[65536]{0:T(1024)S(1)}, f32[65536]{0:T(1024)}, u32[]{:S(2)}) copy-start(f32[65536]{0:T(1024)} %param.14) | copy-start | bytes 786436
  16.7 15.7 %copy-start.2 = (s32[65536]{0:T(1024)S(1)}, s32[65536]{0:T(1024)}, u32[]{:S(2)}) copy-start(s32[65536]{0:T(1024)} %param.15) | copy-start | bytes 786436
  21.2 26.0 %copy-start.4 = (f32[512,128]{1,0:T(8,128)S(1)}, f32[512,128]{1,0:T(8,128)}, u32[]{:S(2)}) copy-start(f32[512,128]{1,0:T(8,128)} %get-tuple-element.18.mid0) | copy-start | bytes 786436
  21.2 25.9 %copy-start.5 = (s32[512,128]{1,0:T(8,128)S(1)}, s32[512,128]{1,0:T(8,128)}, u32[]{:S(2)}) copy-start(s32[512,128]{1,0:T(8,128)} %get-tuple-element.17.spot) | copy-start | bytes 786436
  21.2 25.9 %copy-start.6 = (bf16[512,128]{1,0:T(8,128)(2,1)S(1)}, bf16[512,128]{1,0:T(8,128)(2,1)}, u32[]{:S(2)}) copy-start(bf16[512,128]{1,0:T(8,128)(2,1)} %get-tuple-element.16.hit) | copy-start | bytes 393220
  27.9 19.3 %all-to-all-start.1 = ((f32[128,1,1152]{2,1,0:T(1,128)}), f32[128,1,1152]{2,1,0:T(1,128)S(1)}, u32[]{:S(2)}, u32[]{:S(2)}) async-start(f32[128,1,1152]{2,1,0:T(1,128)} %bitcast.16), calls=%async_computation.1 | async-start | bytes 1179648 | tf_op jit(solution)/shard_map/all_to_all | solution.py:452
  32.4 1.0 %copy-start.3 = (f32[512,128]{1,0:T(8,128)S(1)}, f32[512,128]{1,0:T(8,128)}, u32[]{:S(2)}) copy-start(f32[512,128]{1,0:T(8,128)} %get-tuple-element.15.share) | copy-start | bytes 786436

commit v2 on v1

v2 whole, which is shorter than its diff:
```python
import jax
import jax.numpy as jnp
from jax import lax
from jax.experimental import pallas as pl
from jax.experimental.pallas import tpu as pltpu
from jax.sharding import PartitionSpec as P

SUB = 4
RIVERS = 4
recharge_share = 0.2

W = 128
CHUNK = 128
AHEAD = 3
FIELDS = 7
MB = 1024 * 1024


def gat(values, index):
    return jnp.take_along_axis(values, index, axis=1, mode="promise_in_bounds")


def iota(shape, dim):
    return lax.broadcasted_iota(jnp.int32, shape, dim)


def split3(x):
    hi = x.astype(jnp.bfloat16)
    rest = x - hi.astype(jnp.float32)
    mid = rest.astype(jnp.bfloat16)
    low = (rest - mid.astype(jnp.float32)).astype(jnp.bfloat16)
    return hi, mid, low


def run_all(copies):
    for copy in copies:
        copy.start()
    return copies


def wait_all(copies):
    for copy in copies:
        copy.wait()


def moments_kernel(
    soil, coef, rain, storage, rate, links, owner, reach, volume, lag, send, top, low, low_coef, rain_v, s_v, r_v, to_v, pack_v, sems
):
    lane = iota((W, W), 1)
    sub = iota((W, W), 0)
    pairs = (
        (links, to_v),
        (rate, r_v),
        (storage, s_v),
        (soil.at[:, 0, :], top),
        (soil.at[:, 5, :], low),
        (coef.at[:, 5, :], low_coef),
        (rain, rain_v),
    )
    loads = run_all([pltpu.make_async_copy(src, dst, sems.at[k]) for k, (src, dst) in enumerate(pairs)])

    before = (sub < lane).astype(jnp.bfloat16)
    hits = []
    carry = jnp.zeros((W, 1), jnp.float32)
    for step in range(owner.shape[0]):
        own = jnp.broadcast_to(owner[step : step + 1, :], (W, CHUNK))
        hit = (own == sub).astype(jnp.float32)
        hit16 = hit.astype(jnp.bfloat16)
        hits.append(hit16)
        seen = jnp.dot(hit16, before, preferred_element_type=jnp.float32) + carry
        carry = carry + jnp.sum(hit, axis=1, keepdims=True)
        rank = jnp.sum(hit * seen, axis=0, keepdims=True)
        both = rank + 8.0 * reach[step : step + 1, :].astype(jnp.float32)
        both = jnp.transpose(jnp.broadcast_to(both, (W, CHUNK)))
        pack_v[step * CHUNK : (step + 1) * CHUNK, :] = both
    send[pl.ds(1, W, AHEAD), :] = jnp.broadcast_to(lag[...], (W, W))
    send[pl.ds(2, W, AHEAD), :] = jnp.broadcast_to(volume[...], (W, W))

    field = iota(s_v.shape, 1) & 15
    slot = iota(s_v.shape, 1) >> 4
    both = pack_v[...].astype(jnp.int32)
    out = (both >> 3).astype(jnp.float32)
    total = lambda term: jnp.sum(term, axis=1, keepdims=True)

    wait_all(loads[:2])
    r, down = r_v[...], to_v[...]
    leaves = down == W
    to = down & (W - 1)
    follow = lambda v: jnp.where(leaves, 0.0, gat(v, to))
    a1 = jnp.where(leaves, r, 0.0)
    a2 = a1 * r
    a3 = a2 * r
    g = follow(a1)
    w_1 = r * g
    w_2 = w_1 * g
    w_3 = w_2 * g
    x_1 = r * follow(w_1)
    x_2 = r * follow(w_2)
    z = w_1 * (1.0 - r) + x_1
    y = r * follow(z)
    loads[2].wait()
    s = s_v[...]
    for f, a in enumerate((a1, a2, a3, a3 * r)):
        out = jnp.where(field == f, total(a * s), out)
    wait_all(loads[3:])
    w0, w5 = top[...], low[...]
    share = (rain_v[...] * w0 * w0 + low_coef[...] * w5 * w5 * w5) * (1.0 / SUB)
    e1 = (1.0 - r) * s + share
    h1 = a1 * share
    h2 = a2 * share
    terms = (
        h1 + w_1 * s,
        h2 + w_2 * s,
        a3 * share + w_3 * s,
        h1 + w_1 * e1 + x_1 * s,
        h2 + w_2 * e1 + x_2 * s,
        h1 + w_1 * share + z * e1 + y * s,
    )
    for f, term in enumerate(terms):
        out = jnp.where(field == f + 4, total(term), out)
    out = jnp.where(slot == (both & 7), out, 0.0)
    parts = jnp.concatenate(split3(out), axis=1)
    got = jnp.dot(jnp.concatenate(hits, axis=1), parts, preferred_element_type=jnp.float32)
    send[pl.ds(0, W, AHEAD), :] = got[:, :W] + got[:, W : 2 * W] + got[:, 2 * W :]


def soil_kernel(soil, coef, rain, after, owner, reach, soil_mid, mid0, share, hit, spot, water_v, coef_v, out_v, rain_v, sems, out_sems):
    del after
    layers = water_v.shape[0]
    loads = run_all([pltpu.make_async_copy(rain, rain_v, sems.at[0, layers])])
    for layer in range(layers):
        loads.append(pltpu.make_async_copy(soil.at[:, layer, :], water_v.at[layer], sems.at[0, layer]))
        loads.append(pltpu.make_async_copy(coef.at[:, layer, :], coef_v.at[layer], sems.at[1, layer]))
    run_all(loads[1:])
    sub = iota((W, W), 0)
    for step in range(owner.shape[0]):
        at = slice(step * CHUNK, (step + 1) * CHUNK)
        at_reach = jnp.broadcast_to(reach[step : step + 1, :], (W, CHUNK))
        hit[at, :] = jnp.transpose((at_reach == sub).astype(jnp.float32)).astype(jnp.bfloat16)
        place = jnp.broadcast_to(owner[step : step + 1, :].astype(jnp.float32), (W, CHUNK))
        spot[at, :] = jnp.transpose(place).astype(jnp.int32)
    loads[0].wait()
    stores = []
    coming = surface = None
    for layer in range(layers):
        wait_all(loads[1 + 2 * layer : 3 + 2 * layer])
        water = water_v[layer]
        if layer == 0:
            surface = rain_v[...] * water * water
            coming = rain_v[...] - surface
        drained = coef_v[layer] * water * water * water
        mid = water + coming - drained
        coming = drained
        if layer == 0:
            mid0[...] = mid
        else:
            out_v[layer] = mid
            copy = pltpu.make_async_copy(out_v.at[layer], soil_mid.at[:, layer, :], out_sems.at[layer])
            copy.start()
            stores.append(copy)
    share[...] = (surface + coming) * (1.0 / SUB)
    wait_all(stores)


def sort_columns(v):
    sub = iota((8, W), 0)
    size = 2
    while size <= W:
        j = size // 2
        while j >= 1:
            for a in range(16):
                if j >= 16:
                    d = j >> 4
                    clear = (sub & d) == 0
                    other = jnp.where(clear, pltpu.roll(v[a], 8 - d, 0), pltpu.roll(v[a], d, 0))
                    bit = sub // d & 1
                    lower = bit == (sub // (size >> 4) & 1) if size < W else clear
                    v[a] = jnp.where(lower, jnp.minimum(v[a], other), jnp.maximum(v[a], other))
                elif not a & j:
                    b = a | j
                    low, high = jnp.minimum(v[a], v[b]), jnp.maximum(v[a], v[b])
                    if size < 16:
                        v[a], v[b] = (high, low) if a & size else (low, high)
                    elif size == W:
                        v[a], v[b] = low, high
                    else:
                        up = (sub & (size >> 4)) == 0
                        v[a], v[b] = jnp.where(up, low, high), jnp.where(up, high, low)
            j //= 2
        size *= 2
    return v


def river_tables(recv, tables):
    lag = jnp.transpose(recv[pl.ds(1, W, AHEAD), :])
    volume = jnp.transpose(recv[pl.ds(2, W, AHEAD), :])
    row = iota((W, W), 0)
    weight = 1.0 / (1.0 + lag)
    product = prefix = suffix = weight
    by = 1
    k = 0
    while by < W:
        ok = row >= by
        tables[k] = jnp.where(ok, product, 0.0)
        product = product * pltpu.roll(product, by, 0)
        prefix = prefix * jnp.where(ok, pltpu.roll(prefix, by, 0), 1.0)
        suffix = suffix * jnp.where(row < W - by, pltpu.roll(suffix, W - by, 0), 1.0)
        by *= 2
        k += 1
    for i, value in enumerate((prefix, suffix, weight, lag, volume)):
        tables[k + i] = value
    whole = jnp.transpose(jnp.broadcast_to(prefix[W - 1 : W, :], (W, W)))
    factor = jnp.where(row < W - RIVERS, pltpu.roll(whole, W - RIVERS, 0), 0.0)
    reached = (iota((W, W), 1) == row + RIVERS).astype(jnp.float32)
    by = RIVERS
    while by < W:
        reached = reached + factor * pltpu.roll(reached, W - by, 0)
        factor = factor * pltpu.roll(factor, W - by, 0)
        by *= 2
    for i, part in enumerate(split3(reached)):
        tables[k + 5 + i] = part.astype(jnp.float32)


def inflow_kernel(share, storage, rate, links, recv, gains, tables, key_v, s_v, share_v, sem):
    load = pltpu.make_async_copy(share, share_v, sem)
    load.start()
    shape = storage.shape
    sub = iota((8, W), 0)
    for step in range(shape[0] // CHUNK):
        at = slice(step * CHUNK, (step + 1) * CHUNK)
        turned = jnp.transpose(links[at, :].astype(jnp.float32))
        tiles = [
            turned[8 * a : 8 * a + 8, :] * float(W) + (sub + 8 * a).astype(jnp.float32)
            for a in range(W // 8)
        ]
        key_v[at, :] = jnp.transpose(jnp.concatenate(sort_columns(tiles), axis=0))
    river_tables(recv, tables)

    lane = iota(shape, 1)
    key = key_v[...].astype(jnp.int32)
    order = key & (W - 1)
    dest = key >> 7
    count = jnp.zeros(shape, jnp.int32)
    for shift in (64, 32, 16, 8, 4, 2, 1):
        last = count + (shift - 1)
        found = gat(dest, ((last & 15) << 3) | (last >> 4))
        count = jnp.where(found <= lane, count + shift, count)
    earlier = jnp.where(lane == 0, 0, pltpu.roll(count, 1, 1))
    q = iota((W, W), 0)
    ahead = ((q >> 3) + 16 * (q & 7) < iota((W, W), 1)).astype(jnp.bfloat16)
    ahead = jnp.concatenate([ahead] * 3, axis=0)
    s_v[...] = storage[...]
    load.wait()
    for n in range(SUB):
        s = s_v[...]
        release = rate[...] * s
        parts = jnp.concatenate(split3(gat(release, order)), axis=1)
        run = jnp.dot(parts, ahead, preferred_element_type=jnp.float32)
        gain = share_v[...] + (gat(run, count) - gat(run, earlier))
        gains[n] = gain
        s_v[...] = s + gain - release


def reach_kernel(recv, volume, out):
    got = recv[pl.ds(0, W, AHEAD), :]
    turned = jnp.transpose(got)
    lane = iota((W, W), 1)
    total = jnp.zeros((48, W), jnp.float32)
    for c in range(8):
        at = jnp.broadcast_to(got[:, c * 16 + 10 : c * 16 + 11], (W, W)).astype(jnp.int32)
        hit = (at == lane).astype(jnp.bfloat16)
        parts = jnp.concatenate(split3(turned[c * 16 : c * 16 + 16, :]), axis=0)
        total += jnp.dot(parts, hit, preferred_element_type=jnp.float32)
    total = total[:16, :] + total[16:32, :] + total[32:, :]
    row = lambda f: total[f : f + 1, :]
    vol = volume[...]
    back = 1.0 / (1.0 + vol)
    lateral = back * row(0) * (1.0 / W)
    s1 = row(0) - back * row(1) + row(4)
    s2 = row(1) - back * row(2) + row(5)
    s3 = row(2) - back * row(3) + row(6)
    fields = (lateral, s1, s2, s3, row(7), row(8), row(9))
    wide = [jnp.broadcast_to(value, (8, W)) for value in fields]
    sub = iota((8, W), 0)
    period = []
    for k in range(FIELDS):
        tile = jnp.zeros((8, W), jnp.float32)
        for i in range(8):
            tile = jnp.where(sub == i, wide[(k * 8 + i) % FIELDS], tile)
        period.append(tile)
    for k in range(W // 8):
        for f in range(FIELDS):
            at = (k * FIELDS + f) * 8
            out[at : at + 8, :] = period[f]


def finish_kernel(
    me, fields, tables, gains, storage, rate, links, hit, spot, mid0, soil_mid, soil_out, storage_out, section,
    table, flow_ref, g_v, s_v, r_v, to_v, hit_v, spot_v, mid_v, out_v, top_v, sems, out_sems
):
    del soil_mid
    loads = run_all(
        [
            pltpu.make_async_copy(src, dst, sems.at[k])
            for k, (src, dst) in enumerate(
                (
                    (hit, hit_v),
                    (spot, spot_v),
                    (storage, s_v),
                    (rate, r_v),
                    (links, to_v),
                    (gains, g_v),
                    (mid0, mid_v),
                )
            )
        ]
    )
    field = lambda f: jnp.transpose(fields[pl.ds(f, W, FIELDS), :])
    levels = 7
    prefix, suffix, weight, lag, volume = (tables[levels + k] for k in range(5))
    crossing = jnp.concatenate([tables[levels + 5 + k].astype(jnp.bfloat16) for k in range(3)], axis=1)
    lateral = field(0)
    s1, s2, s3 = field(1), field(2), field(3)
    c11, c12, c21 = field(4), field(5), field(6)
    flow = volume
    for n in range(SUB):
        back = 1.0 / (1.0 + volume)
        for part, value in enumerate(split3(back)):
            table[:, (part * SUB + n) * W : (part * SUB + n + 1) * W] = value
        if n == 1:
            lateral = back * s1 * (1.0 / W)
            s1, s2 = s1 - back * s2 + c11, s2 - back * s3 + c12
        elif n == 2:
            lateral = back * s1 * (1.0 / W)
            s1 = s1 - back * s2 + c21
        elif n == 3:
            lateral = back * s1 * (1.0 / W)
        entering = volume + lateral
        ends = jnp.sum(entering * suffix, axis=0, keepdims=True)
        ends = jnp.concatenate([jnp.broadcast_to(part, (16, W)) for part in split3(ends)], axis=0)
        head = jnp.dot(ends, crossing, preferred_element_type=jnp.float32)
        head = head[:8, :] + head[16:24, :] + head[32:40, :]
        head = head[:1, :W] + head[:1, W : 2 * W] + head[:1, 2 * W :]
        run = weight * entering
        for k in range(levels):
            run = run + tables[k] * pltpu.roll(run, 1 << k, 0)
        flow = run + prefix * head
        volume = lag * flow
    flow_ref[...] = jnp.transpose(flow)
    section[...] = jnp.log1p(flow_ref[pl.ds(me[0], 1), :])

    wait_all(loads)
    stores = []
    blocks = s_v.shape[0]
    for step in range(blocks // CHUNK):
        at = slice(step * CHUNK, (step + 1) * CHUNK)
        got = jnp.dot(hit_v[at, :], table[...], preferred_element_type=jnp.float32)
        place = spot_v[at, :]
        s, r = s_v[at, :], r_v[at, :]
        leaves = to_v[at, :] == W
        for n in range(SUB):
            part = lambda k: got[:, (k * SUB + n) * W : (k * SUB + n + 1) * W]
            back = gat(part(0) + part(1) + part(2), place)
            s = s - r * jnp.where(leaves, back, 1.0) * s + g_v[n, at, :]
        out_v[at, :] = s
        top = mid_v[at, :]
        top_v[at, :] = top + recharge_share * (s / (s + 1.0)) * (1.0 - top)
        where = pl.ds(step * CHUNK, CHUNK)
        stores += run_all(
            [
                pltpu.make_async_copy(out_v.at[where], storage_out.at[where], out_sems.at[0, step]),
                pltpu.make_async_copy(top_v.at[where], soil_out.at[where, 0, :], out_sems.at[1, step]),
            ]
        )
    wait_all(stores)


def local(
    soil_water,
    rainfall,
    drain_coef,
    cell_storage,
    release_rate,
    downstream,
    block_owner,
    outlet_reach,
    river_storage,
    river_lag,
):
    axes = ("tile", "grp")
    blocks = block_owner.shape[0]
    steps = blocks // CHUNK
    layers = soil_water.shape[0]

    def tiles(x):
        return x.reshape(layers, blocks, W).transpose(1, 0, 2)

    soil, coef = tiles(soil_water), tiles(drain_coef)
    rain, storage, rate, links = (
        x.reshape(blocks, W) for x in (rainfall, cell_storage, release_rate, downstream)
    )
    owner = block_owner.reshape(steps, CHUNK)
    reach = outlet_reach.reshape(steps, CHUNK)

    f32 = jnp.float32
    i32 = jnp.int32
    b16 = jnp.bfloat16
    shaped = jax.ShapeDtypeStruct
    vmem = pl.BlockSpec(memory_space=pltpu.VMEM)
    hbm = pl.BlockSpec(memory_space=pltpu.HBM)
    params = pltpu.CompilerParams(vmem_limit_bytes=24 * MB)
    scratch = lambda dtype, *shape: pltpu.VMEM(shape, dtype)
    flat = lambda dtype: scratch(dtype, blocks, W)
    stay = lambda x: pltpu.with_memory_space_constraint(x, pltpu.HBM)
    sems = lambda *shape: pltpu.SemaphoreType.DMA(shape)
    cost = lambda flops, moved: pl.CostEstimate(flops=flops, bytes_accessed=moved, transcendentals=0)

    send = pl.pallas_call(
        moments_kernel,
        in_specs=[hbm] * 6 + [vmem] * 4,
        out_specs=vmem,
        out_shape=shaped((W * AHEAD, W), f32),
        scratch_shapes=[flat(f32)] * 6 + [flat(i32), flat(f32), sems(7)],
        compiler_params=params,
        name="moments",
    )(*map(stay, (soil, coef, rain, storage, rate, links, owner, reach, river_storage, river_lag)))

    def exchange(rows, count):
        rows = rows.reshape(W, 1, count * W)
        rows = lax.all_to_all(rows, axes, split_axis=0, concat_axis=0, tiled=True)
        return rows.reshape(W * count, W)

    recv = exchange(send, AHEAD)

    soil_mid, mid0, share, hit, spot = pl.pallas_call(
        soil_kernel,
        in_specs=[hbm] * 4 + [vmem] * 2,
        out_specs=[hbm] + [vmem] * 4,
        out_shape=[
            pltpu.HBM((blocks, layers, W), f32),
            pltpu.HBM((blocks, W), f32),
            pltpu.HBM((blocks, W), f32),
            pltpu.HBM((blocks, W), b16),
            pltpu.HBM((blocks, W), i32),
        ],
        scratch_shapes=[scratch(f32, layers, blocks, W)] * 3 + [flat(f32), sems(2, layers + 1), sems(layers)],
        compiler_params=params,
        cost_estimate=cost(3_000_000, 10 * MB),
        name="soil",
    )(*map(stay, (soil, coef, rain, send, owner, reach)))

    recv, spot = lax.optimization_barrier((recv, spot))

    fields = pl.pallas_call(
        reach_kernel,
        in_specs=[vmem] * 2,
        out_specs=vmem,
        out_shape=shaped((W * FIELDS, W), f32),
        compiler_params=params,
        name="reaches",
    )(recv, river_storage)
    fields, recv = lax.optimization_barrier((fields, recv))
    fields = exchange(fields, FIELDS)

    gains, tables = pl.pallas_call(
        inflow_kernel,
        in_specs=[hbm] + [vmem] * 4,
        out_specs=[vmem] * 2,
        out_shape=[shaped((SUB, blocks, W), f32), shaped((15, W, W), f32)],
        scratch_shapes=[flat(f32)] * 3 + [pltpu.SemaphoreType.DMA],
        compiler_params=params,
        cost_estimate=cost(10_000_000, 16 * MB),
        name="inflow",
    )(stay(share), storage, rate, links, recv)

    me = lax.axis_index(axes).astype(jnp.int32).reshape(1)
    soil_out, storage_out, section = pl.pallas_call(
        finish_kernel,
        in_specs=[pl.BlockSpec(memory_space=pltpu.SMEM)] + [vmem] * 2 + [hbm] * 8,
        out_specs=[hbm, hbm, vmem],
        out_shape=[
            shaped((blocks, layers, W), f32),
            shaped((blocks, W), f32),
            shaped((1, W), f32),
        ],
        scratch_shapes=[
            scratch(b16, W, 3 * SUB * W),
            scratch(f32, W, W),
            scratch(f32, SUB, blocks, W),
            flat(f32),
            flat(f32),
            flat(i32),
            flat(b16),
            flat(i32),
            flat(f32),
            flat(f32),
            flat(f32),
            sems(7),
            sems(2, steps),
        ],
        input_output_aliases={10: 0},
        compiler_params=params,
        name="finish",
    )(me, fields, tables, gains, *map(stay, (storage, rate, links, hit, spot, mid0, soil_mid)))

    soil_out = soil_out.transpose(1, 0, 2).reshape(layers, blocks * W)
    return (soil_out, storage_out.reshape(-1), section)


def solution(mesh):
    placed = (
        P(None, ("tile", "grp")),
        P(("tile", "grp")),
        P(None, ("tile", "grp")),
        P(("tile", "grp")),
        P(("tile", "grp")),
        P(("tile", "grp")),
        P(("tile", "grp"), None),
        P(("tile", "grp")),
        P("grp", "tile"),
        P("grp", "tile"),
    )
    return jax.shard_map(
        local,
        mesh=mesh,
        in_specs=placed,
        out_specs=(P(None, ("tile", "grp")), P(("tile", "grp")), P("grp", "tile")),
        check_vma=False,
    )
```

time: 52.6 us -> 50.2 us (0.954)
  Pallas kernels: 21.7 us -> 18.6 us
  waiting for transfers between devices: 12.7 us -> 15 us
  local copies, waits for them, and re-layouts: 0.99 us -> 0.03 us
    all_to_all x2, waiting for transfers between devices: 12.7 us -> 15 us  [exchange(): rows = lax.all_to_all(rows, axes, split_axis=0, concat_axis=0, tiled=True)]
    pallas_call x3, Pallas kernels: 12.2 us -> 10 us  [the longest x1 4.39 us: local(): pl.pallas_call(inflow_kernel, in_specs=[hbm] + [vmem] * 4, out_specs=[vme...]
    unnamed x18 -> x8, local copies, waits for them, and re-layouts: 0.99 us -> 0.03 us
    pallas_call x1, Pallas kernels: 4.99 us -> 4.05 us  [local(): pl.pallas_call(finish_kernel, in_specs=[pl.BlockSpec(memory_space=pltpu.S...]
  transfers between devices with their start and end apart: 2 -> 2, of which waited for: 2 -> 2; matrix products, arithmetic and copies ran while one was open for 0% -> 0% of each run, Pallas kernels for 21% -> 18%
where the time goes in v2:
time: 50.2 us; the launch traced here: 49.9 us
  Pallas kernels  18.6 us (37%)
  starting transfers between devices  15.5 us (31%)
  waiting for transfers between devices  15 us (30%)
  between operations  0.73 us (1%)
    all_to_all x2, starting transfers between devices, exchange(): rows = lax.all_to_all(rows, axes, split_axis=0, concat_axis=0, tiled=True)  15.5 us
    all_to_all x2, waiting for transfers between devices, exchange(): rows = lax.all_to_all(rows, axes, split_axis=0, concat_axis=0, tiled=True)  15 us
    pallas_call x1, Pallas kernels, local(): pl.pallas_call(soil_kernel, in_specs=[hbm] * 4 + [vmem] * 2, out_specs=[h...  4.51 us
    pallas_call x1, Pallas kernels, local(): pl.pallas_call(inflow_kernel, in_specs=[hbm] + [vmem] * 4, out_specs=[vme...  4.39 us
    pallas_call x1, Pallas kernels, local(): pl.pallas_call(moments_kernel, in_specs=[hbm] * 6 + [vmem] * 4, out_specs...  4.38 us
    pallas_call x1, Pallas kernels, local(): pl.pallas_call(finish_kernel, in_specs=[pl.BlockSpec(memory_space=pltpu.S...  4.05 us
    pallas_call x1, Pallas kernels, local(): pl.pallas_call(reach_kernel, in_specs=[vmem] * 2, out_specs=vmem, out_sha...  1.24 us
  transfers between devices with their start and end apart: 2, of which 2 were waited for; matrix products, arithmetic and copies ran while one was open for 0% of the time, Pallas kernels for 18%

profile of v2, /device:TPU:1, one launch (start us, length us, event | category | flops | bytes accessed | tf_op | source)
XLA Modules:
  0.0 49.9 jit_solution(2327953514692029093)
XLA Ops:
  0.6 4.4 %moments.1.after = f32[384,128]{1,0:T(8,128)} custom-call(f32[512,6,128]{2,1,0:T(8,128)} %bitcast.33, f32[512,6,128]{2,1,0:T(8,128)} %bitcast.35, f32[512,128]{1,0:T(8,128)} %bitcast.38, f32[512,128]{1,0:T(8,128)} %bitcast.21, f32[512,128]{1,0:T(8,128)} %bitcast.24, s32[512,128]{1,0:T(8,128)} %bitcast.27, s32[4,128]{1,0:T(4,128)} %bitcast.40, ...), custom_call_target="tpu_custom_call" | custom-call | tf_op jit(solution)/shard_map/moments/pallas_call | solution.py:418
  5.0 11.5 %all-to-all-start = ((f32[128,1,384]{2,1,0:T(1,128)}), f32[128,1,384]{2,1,0:T(1,128)S(1)}, u32[]{:S(2)}, u32[]{:S(2)}) async-start(f32[128,1,384]{2,1,0:T(1,128)} %bitcast.11), calls=%async_computation | async-start | bytes 393216 | tf_op jit(solution)/shard_map/all_to_all | solution.py:430
  16.5 0.0 copy-start.3
  16.5 0.0 copy-start
  16.5 0.0 copy-start.1
  16.6 0.0 copy-start.2
  16.6 4.5 %soil.1 = (f32[512,6,128]{2,1,0:T(8,128)}, f32[512,128]{1,0:T(8,128)}, f32[512,128]{1,0:T(8,128)}, bf16[512,128]{1,0:T(8,128)(2,1)}, s32[512,128]{1,0:T(8,128)}) custom-call(f32[512,6,128]{2,1,0:T(8,128)} %bitcast.34, f32[512,6,128]{2,1,0:T(8,128)} %bitcast.36, f32[512,128]{1,0:T(8,128)} %bitcast.39, f32[384,128]{1,0:T(8,128)} %moments.1.after, ...), custom_call_target="tpu_custom_call" | custom-call | flops 3000000 | bytes 10485760 | tf_op jit(solution)/shard_map/soil/pallas_call | solution.py:435
  21.1 6.0 %all-to-all-done = f32[128,1,384]{2,1,0:T(1,128)S(1)} async-done(((f32[128,1,384]{2,1,0:T(1,128)}), f32[128,1,384]{2,1,0:T(1,128)S(1)}, u32[]{:S(2)}, u32[]{:S(2)}) %all-to-all-start) | async-done | bytes 196640 | tf_op jit(solution)/shard_map/all_to_all | solution.py:430
  27.1 0.0 copy-done.3
  27.1 1.2 %reaches.1 = f32[896,128]{1,0:T(8,128)} custom-call(f32[384,128]{1,0:T(8,128)S(1)} %bitcast.31, f32[1,128]{1,0:T(1,128)S(1)} %copy-done.3), custom_call_target="tpu_custom_call" | custom-call | tf_op jit(solution)/shard_map/reaches/pallas_call | solution.py:454
  28.4 4.0 %all-to-all-start.1 = ((f32[128,1,896]{2,1,0:T(1,128)}), f32[128,1,896]{2,1,0:T(1,128)S(1)}, u32[]{:S(2)}, u32[]{:S(2)}) async-start(f32[128,1,896]{2,1,0:T(1,128)} %bitcast.15), calls=%async_computation.1 | async-start | bytes 917504 | tf_op jit(solution)/shard_map/all_to_all | solution.py:430
  32.4 0.0 copy-done
  32.4 0.0 copy-done.1
  32.4 0.0 copy-done.2
  32.5 4.4 %inflow.1 = (f32[4,512,128]{2,1,0:T(8,128)S(1)}, f32[15,128,128]{2,1,0:T(8,128)S(1)}) custom-call(f32[512,128]{1,0:T(8,128)} %get-tuple-element.20.share, f32[512,128]{1,0:T(8,128)S(1)} %bitcast.23, f32[512,128]{1,0:T(8,128)S(1)} %bitcast.26, s32[512,128]{1,0:T(8,128)S(1)} %bitcast.29, f32[384,128]{1,0:T(8,128)S(1)} %bitcast.32), custom_call_target="tpu_custom_call" | custom-call | flops 10000000 | bytes 16777216 | tf_op jit(solution)/shard_map/inflow/pallas_call | solution.py:465
  36.9 9.0 %all-to-all-done.1 = f32[128,1,896]{2,1,0:T(1,128)S(1)} async-done(((f32[128,1,896]{2,1,0:T(1,128)}), f32[128,1,896]{2,1,0:T(1,128)S(1)}, u32[]{:S(2)}, u32[]{:S(2)}) %all-to-all-start.1) | async-done | bytes 458784 | tf_op jit(solution)/shard_map/all_to_all | solution.py:430
  45.8 4.0 %finish.1 = (f32[512,6,128]{2,1,0:T(8,128)}, f32[512,128]{1,0:T(8,128)}, f32[1,128]{1,0:T(1,128)}) custom-call(s32[1]{0:T(128)} %bitcast.me, f32[896,128]{1,0:T(8,128)S(1)} %bitcast.30, f32[15,128,128]{2,1,0:T(8,128)S(1)} %get-tuple-element.22.tables, f32[4,512,128]{2,1,0:T(8,128)S(1)} %get-tuple-element.23.gains, ...), custom_call_target="tpu_custom_call", output_to_operand_aliasing={{0}: (10, {})} | custom-call | tf_op jit(solution)/shard_map/finish/pallas_call | solution.py:477
Async XLA Ops:
  5.0 22.1 %all-to-all-start = ((f32[128,1,384]{2,1,0:T(1,128)}), f32[128,1,384]{2,1,0:T(1,128)S(1)}, u32[]{:S(2)}, u32[]{:S(2)}) async-start(f32[128,1,384]{2,1,0:T(1,128)} %bitcast.11), calls=%async_computation | async-start | bytes 393216 | tf_op jit(solution)/shard_map/all_to_all | solution.py:430
  16.5 10.6 %copy-start.3 = (f32[1,128]{1,0:T(1,128)S(1)}, f32[1,128]{1,0:T(1,128)}, u32[]{:S(2)}) copy-start(f32[1,128]{1,0:T(1,128)} %volume.3) | copy-start | bytes 1540
  16.5 15.9 %copy-start = (f32[65536]{0:T(1024)S(1)}, f32[65536]{0:T(1024)}, u32[]{:S(2)}) copy-start(f32[65536]{0:T(1024)} %param.13) | copy-start | bytes 786436
  16.5 15.9 %copy-start.1 = (f32[65536]{0:T(1024)S(1)}, f32[65536]{0:T(1024)}, u32[]{:S(2)}) copy-start(f32[65536]{0:T(1024)} %param.14) | copy-start | bytes 786436
  16.6 15.9 %copy-start.2 = (s32[65536]{0:T(1024)S(1)}, s32[65536]{0:T(1024)}, u32[]{:S(2)}) copy-start(s32[65536]{0:T(1024)} %param.15) | copy-start | bytes 786436
  28.4 17.5 %all-to-all-start.1 = ((f32[128,1,896]{2,1,0:T(1,128)}), f32[128,1,896]{2,1,0:T(1,128)S(1)}, u32[]{:S(2)}, u32[]{:S(2)}) async-start(f32[128,1,896]{2,1,0:T(1,128)} %bitcast.15), calls=%async_computation.1 | async-start | bytes 917504 | tf_op jit(solution)/shard_map/all_to_all | solution.py:430

commit v3 on v2

--- a/solution.py
+++ b/solution.py
@@ -44,11 +44,16 @@
 
 
 def moments_kernel(
-    soil, coef, rain, storage, rate, links, owner, reach, volume, lag, send, top, low, low_coef, rain_v, s_v, r_v, to_v, pack_v, sems
+    soil, coef, rain, storage, rate, links, owner_hbm, reach_hbm, volume_hbm, lag_hbm, send,
+    top, low, low_coef, rain_v, s_v, r_v, to_v, pack_v, owner, reach, volume, lag, sems
 ):
     lane = iota((W, W), 1)
     sub = iota((W, W), 0)
     pairs = (
+        (owner_hbm, owner),
+        (reach_hbm, reach),
+        (volume_hbm, volume),
+        (lag_hbm, lag),
         (links, to_v),
         (rate, r_v),
         (storage, s_v),
@@ -59,6 +64,8 @@
     )
     loads = run_all([pltpu.make_async_copy(src, dst, sems.at[k]) for k, (src, dst) in enumerate(pairs)])
 
+    small, loads = loads[:4], loads[4:]
+    wait_all(small)
     before = (sub < lane).astype(jnp.bfloat16)
     hits = []
     carry = jnp.zeros((W, 1), jnp.float32)
@@ -221,9 +228,11 @@
         tables[k + 5 + i] = part.astype(jnp.float32)
 
 
-def inflow_kernel(share, storage, rate, links, recv, gains, tables, key_v, s_v, share_v, sem):
-    load = pltpu.make_async_copy(share, share_v, sem)
-    load.start()
+def inflow_kernel(
+    share, hit, spot, storage, rate, links, recv, gains, tables, key_v, s_v, share_v, hit_v, spot_v, sems
+):
+    pairs = ((share, share_v), (hit, hit_v), (spot, spot_v))
+    loads = run_all([pltpu.make_async_copy(src, dst, sems.at[k]) for k, (src, dst) in enumerate(pairs)])
     shape = storage.shape
     sub = iota((8, W), 0)
     for step in range(shape[0] // CHUNK):
@@ -250,14 +259,20 @@
     ahead = ((q >> 3) + 16 * (q & 7) < iota((W, W), 1)).astype(jnp.bfloat16)
     ahead = jnp.concatenate([ahead] * 3, axis=0)
     s_v[...] = storage[...]
-    load.wait()
+    wait_all(loads)
     for n in range(SUB):
         s = s_v[...]
         release = rate[...] * s
         parts = jnp.concatenate(split3(gat(release, order)), axis=1)
         run = jnp.dot(parts, ahead, preferred_element_type=jnp.float32)
         gain = share_v[...] + (gat(run, count) - gat(run, earlier))
-        gains[n] = gain
+        if n == 0:
+            parts = jnp.concatenate(split3(1.0 / (1.0 + tables[11])), axis=1)
+            seen = jnp.dot(hit_v[...], parts, preferred_element_type=jnp.float32)
+            back = gat(seen[:, :W] + seen[:, W : 2 * W] + seen[:, 2 * W :], spot_v[...])
+            gains[n] = s - release * jnp.where(links[...] == W, back, 1.0) + gain
+        else:
+            gains[n] = gain
         s_v[...] = s + gain - release
 
 
@@ -295,8 +310,8 @@
 
 
 def finish_kernel(
-    me, fields, tables, gains, storage, rate, links, hit, spot, mid0, soil_mid, soil_out, storage_out, section,
-    table, flow_ref, g_v, s_v, r_v, to_v, hit_v, spot_v, mid_v, out_v, top_v, sems, out_sems
+    fields, tables, gains, rate, links, hit, spot, mid0, soil_mid, soil_out, storage_out, section,
+    table, flow_ref, hit_v, spot_v, mid_v, out_v, top_v, section_v, sems, out_sems, section_sem
 ):
     del soil_mid
     loads = run_all(
@@ -306,10 +321,6 @@
                 (
                     (hit, hit_v),
                     (spot, spot_v),
-                    (storage, s_v),
-                    (rate, r_v),
-                    (links, to_v),
-                    (gains, g_v),
                     (mid0, mid_v),
                 )
             )
@@ -324,9 +335,11 @@
     c11, c12, c21 = field(4), field(5), field(6)
     flow = volume
     for n in range(SUB):
-        back = 1.0 / (1.0 + volume)
-        for part, value in enumerate(split3(back)):
-            table[:, (part * SUB + n) * W : (part * SUB + n + 1) * W] = value
+        if n:
+            back = 1.0 / (1.0 + volume)
+            for part, value in enumerate(split3(back)):
+                at = (part * (SUB - 1) + n - 1) * W
+                table[:, at : at + W] = value
         if n == 1:
             lateral = back * s1 * (1.0 / W)
             s1, s2 = s1 - back * s2 + c11, s2 - back * s3 + c12
@@ -346,22 +359,21 @@
             run = run + tables[k] * pltpu.roll(run, 1 << k, 0)
         flow = run + prefix * head
         volume = lag * flow
-    flow_ref[...] = jnp.transpose(flow)
-    section[...] = jnp.log1p(flow_ref[pl.ds(me[0], 1), :])
+    flow_ref[...] = flow
 
     wait_all(loads)
     stores = []
-    blocks = s_v.shape[0]
+    blocks = out_v.shape[0]
     for step in range(blocks // CHUNK):
         at = slice(step * CHUNK, (step + 1) * CHUNK)
         got = jnp.dot(hit_v[at, :], table[...], preferred_element_type=jnp.float32)
         place = spot_v[at, :]
-        s, r = s_v[at, :], r_v[at, :]
-        leaves = to_v[at, :] == W
-        for n in range(SUB):
-            part = lambda k: got[:, (k * SUB + n) * W : (k * SUB + n + 1) * W]
+        s, r = gains[0, at, :], rate[at, :]
+        leaves = links[at, :] == W
+        for n in range(1, SUB):
+            part = lambda k: got[:, (k * (SUB - 1) + n - 1) * W : (k * (SUB - 1) + n) * W]
             back = gat(part(0) + part(1) + part(2), place)
-            s = s - r * jnp.where(leaves, back, 1.0) * s + g_v[n, at, :]
+            s = s - r * jnp.where(leaves, back, 1.0) * s + gains[n, at, :]
         out_v[at, :] = s
         top = mid_v[at, :]
         top_v[at, :] = top + recharge_share * (s / (s + 1.0)) * (1.0 - top)
@@ -372,6 +384,10 @@
                 pltpu.make_async_copy(top_v.at[where], soil_out.at[where, 0, :], out_sems.at[1, step]),
             ]
         )
+        if step == 1:
+            flow_ref[...] = jnp.transpose(flow_ref[...])
+            section_v[...] = jnp.log1p(flow_ref[pl.ds(lax.axis_index(("tile", "grp")), 1), :])
+            stores += run_all([pltpu.make_async_copy(section_v, section, section_sem)])
     wait_all(stores)
 
 
@@ -417,10 +433,14 @@
 
     send = pl.pallas_call(
         moments_kernel,
-        in_specs=[hbm] * 6 + [vmem] * 4,
+        in_specs=[hbm] * 10,
         out_specs=vmem,
         out_shape=shaped((W * AHEAD, W), f32),
-        scratch_shapes=[flat(f32)] * 6 + [flat(i32), flat(f32), sems(7)],
+        scratch_shapes=[flat(f32)] * 6
+        + [flat(i32), flat(f32)]
+        + [scratch(i32, steps, CHUNK)] * 2
+        + [scratch(f32, 1, W)] * 2
+        + [sems(11)],
         compiler_params=params,
         name="moments",
     )(*map(stay, (soil, coef, rain, storage, rate, links, owner, reach, river_storage, river_lag)))
@@ -464,44 +484,41 @@
 
     gains, tables = pl.pallas_call(
         inflow_kernel,
-        in_specs=[hbm] + [vmem] * 4,
+        in_specs=[hbm] * 3 + [vmem] * 4,
         out_specs=[vmem] * 2,
         out_shape=[shaped((SUB, blocks, W), f32), shaped((15, W, W), f32)],
-        scratch_shapes=[flat(f32)] * 3 + [pltpu.SemaphoreType.DMA],
+        scratch_shapes=[flat(f32)] * 3 + [flat(b16), flat(i32), sems(3)],
         compiler_params=params,
         cost_estimate=cost(10_000_000, 16 * MB),
         name="inflow",
-    )(stay(share), storage, rate, links, recv)
-
-    me = lax.axis_index(axes).astype(jnp.int32).reshape(1)
+    )(*map(stay, (share, hit, spot)), storage, rate, links, recv)
+
     soil_out, storage_out, section = pl.pallas_call(
         finish_kernel,
-        in_specs=[pl.BlockSpec(memory_space=pltpu.SMEM)] + [vmem] * 2 + [hbm] * 8,
-        out_specs=[hbm, hbm, vmem],
+        in_specs=[vmem] * 5 + [hbm] * 4,
+        out_specs=[hbm] * 3,
         out_shape=[
             shaped((blocks, layers, W), f32),
             shaped((blocks, W), f32),
             shaped((1, W), f32),
         ],
         scratch_shapes=[
-            scratch(b16, W, 3 * SUB * W),
+            scratch(b16, W, 3 * (SUB - 1) * W),
             scratch(f32, W, W),
-            scratch(f32, SUB, blocks, W),
-            flat(f32),
-            flat(f32),
-            flat(i32),
             flat(b16),
             flat(i32),
             flat(f32),
             flat(f32),
             flat(f32),
-            sems(7),
+            scratch(f32, 1, W),
+            sems(3),
             sems(2, steps),
+            pltpu.SemaphoreType.DMA,
         ],
-        input_output_aliases={10: 0},
+        input_output_aliases={8: 0},
         compiler_params=params,
         name="finish",
-    )(me, fields, tables, gains, *map(stay, (storage, rate, links, hit, spot, mid0, soil_mid)))
+    )(fields, tables, gains, rate, links, *map(stay, (hit, spot, mid0, soil_mid)))
 
     soil_out = soil_out.transpose(1, 0, 2).reshape(layers, blocks * W)
     return (soil_out, storage_out.reshape(-1), section)

time: 50.2 us -> 48.1 us (0.958)
  Pallas kernels: 18.6 us -> 16.8 us
    pallas_call x3, Pallas kernels: 12.8 us -> 11.1 us  [the longest x1 4.71 us: local(): pl.pallas_call(inflow_kernel, in_specs=[hbm] * 3 + [vmem] * 4, out_specs=...]
  transfers between devices with their start and end apart: 2 -> 2, of which waited for: 2 -> 2; matrix products, arithmetic and copies ran while one was open for 0% -> 0% of each run, Pallas kernels for 18% -> 19%
where the time goes in v3:
time: 48.1 us; the launch traced here: 47.8 us
  Pallas kernels  16.8 us (35%)
  starting transfers between devices  15.5 us (32%)
  waiting for transfers between devices  14.7 us (31%)
  between operations  0.73 us (2%)
    all_to_all x2, starting transfers between devices, exchange(): rows = lax.all_to_all(rows, axes, split_axis=0, concat_axis=0, tiled=True)  15.5 us
    all_to_all x2, waiting for transfers between devices, exchange(): rows = lax.all_to_all(rows, axes, split_axis=0, concat_axis=0, tiled=True)  14.7 us
    pallas_call x1, Pallas kernels, local(): pl.pallas_call(inflow_kernel, in_specs=[hbm] * 3 + [vmem] * 4, out_specs=...  4.71 us
    pallas_call x1, Pallas kernels, local(): pl.pallas_call(soil_kernel, in_specs=[hbm] * 4 + [vmem] * 2, out_specs=[h...  4.51 us
    pallas_call x1, Pallas kernels, local(): pl.pallas_call(moments_kernel, in_specs=[hbm] * 10, out_specs=vmem, out_s...  3.77 us
    pallas_call x1, Pallas kernels, local(): pl.pallas_call(finish_kernel, in_specs=[vmem] * 5 + [hbm] * 4, out_specs=...  2.59 us
    pallas_call x1, Pallas kernels, local(): pl.pallas_call(reach_kernel, in_specs=[vmem] * 2, out_specs=vmem, out_sha...  1.24 us
  transfers between devices with their start and end apart: 2, of which 2 were waited for; matrix products, arithmetic and copies ran while one was open for 0% of the time, Pallas kernels for 19%

profile of v3, /device:TPU:1, one launch (start us, length us, event | category | flops | bytes accessed | tf_op | source)
XLA Modules:
  0.0 47.8 jit_solution(87876619822989253)
XLA Ops:
  0.6 3.8 %moments.1.after = f32[384,128]{1,0:T(8,128)} custom-call(f32[512,6,128]{2,1,0:T(8,128)} %bitcast.31, f32[512,6,128]{2,1,0:T(8,128)} %bitcast.33, f32[512,128]{1,0:T(8,128)} %bitcast.36, f32[512,128]{1,0:T(8,128)} %bitcast.29, f32[512,128]{1,0:T(8,128)} %bitcast.20, s32[512,128]{1,0:T(8,128)} %bitcast.23, s32[4,128]{1,0:T(4,128)} %bitcast.38, ...), custom_call_target="tpu_custom_call" | custom-call | tf_op jit(solution)/shard_map/moments/pallas_call | solution.py:434
  4.4 11.5 %all-to-all-start = ((f32[128,1,384]{2,1,0:T(1,128)}), f32[128,1,384]{2,1,0:T(1,128)S(1)}, u32[]{:S(2)}, u32[]{:S(2)}) async-start(f32[128,1,384]{2,1,0:T(1,128)} %bitcast.10), calls=%async_computation | async-start | bytes 393216 | tf_op jit(solution)/shard_map/all_to_all | solution.py:450
  15.9 0.0 copy-start.3
  15.9 0.0 copy-start
  15.9 0.0 copy-start.1
  15.9 0.0 copy-start.2
  16.0 4.5 %soil.1 = (f32[512,6,128]{2,1,0:T(8,128)}, f32[512,128]{1,0:T(8,128)}, f32[512,128]{1,0:T(8,128)}, bf16[512,128]{1,0:T(8,128)(2,1)}, s32[512,128]{1,0:T(8,128)}) custom-call(f32[512,6,128]{2,1,0:T(8,128)} %bitcast.32, f32[512,6,128]{2,1,0:T(8,128)} %bitcast.34, f32[512,128]{1,0:T(8,128)} %bitcast.37, f32[384,128]{1,0:T(8,128)} %moments.1.after, ...), custom_call_target="tpu_custom_call" | custom-call | flops 3000000 | bytes 10485760 | tf_op jit(solution)/shard_map/soil/pallas_call | solution.py:455
  20.5 6.0 %all-to-all-done = f32[128,1,384]{2,1,0:T(1,128)S(1)} async-done(((f32[128,1,384]{2,1,0:T(1,128)}), f32[128,1,384]{2,1,0:T(1,128)S(1)}, u32[]{:S(2)}, u32[]{:S(2)}) %all-to-all-start) | async-done | bytes 196640 | tf_op jit(solution)/shard_map/all_to_all | solution.py:450
  26.5 0.0 copy-done.3
  26.5 1.2 %reaches.1 = f32[896,128]{1,0:T(8,128)} custom-call(f32[384,128]{1,0:T(8,128)S(1)} %bitcast.27, f32[1,128]{1,0:T(1,128)S(1)} %copy-done.3), custom_call_target="tpu_custom_call" | custom-call | tf_op jit(solution)/shard_map/reaches/pallas_call | solution.py:474
  27.8 4.0 %all-to-all-start.1 = ((f32[128,1,896]{2,1,0:T(1,128)}), f32[128,1,896]{2,1,0:T(1,128)S(1)}, u32[]{:S(2)}, u32[]{:S(2)}) async-start(f32[128,1,896]{2,1,0:T(1,128)} %bitcast.14), calls=%async_computation.1 | async-start | bytes 917504 | tf_op jit(solution)/shard_map/all_to_all | solution.py:450
  31.8 0.0 copy-done
  31.8 0.0 copy-done.1
  31.8 0.0 copy-done.2
  31.8 4.7 %inflow.1 = (f32[4,512,128]{2,1,0:T(8,128)S(1)}, f32[15,128,128]{2,1,0:T(8,128)S(1)}) custom-call(f32[512,128]{1,0:T(8,128)} %get-tuple-element.20.share, bf16[512,128]{1,0:T(8,128)(2,1)} %get-tuple-element.21.hit, s32[512,128]{1,0:T(8,128)} %get-tuple-element.22.spot, f32[512,128]{1,0:T(8,128)S(1)} %bitcast.30, f32[512,128]{1,0:T(8,128)S(1)} %bitcast.21, ...), custom_call_target="tpu_custom_call" | custom-call | flops 10000000 | bytes 16777216 | tf_op jit(solution)/shard_map/inflow/pallas_call | solution.py:485
  36.6 8.7 %all-to-all-done.1 = f32[128,1,896]{2,1,0:T(1,128)S(1)} async-done(((f32[128,1,896]{2,1,0:T(1,128)}), f32[128,1,896]{2,1,0:T(1,128)S(1)}, u32[]{:S(2)}, u32[]{:S(2)}) %all-to-all-start.1) | async-done | bytes 458784 | tf_op jit(solution)/shard_map/all_to_all | solution.py:450
  45.2 2.6 %finish.1 = (f32[512,6,128]{2,1,0:T(8,128)}, f32[512,128]{1,0:T(8,128)}, f32[1,128]{1,0:T(1,128)}) custom-call(f32[896,128]{1,0:T(8,128)S(1)} %bitcast.26, f32[15,128,128]{2,1,0:T(8,128)S(1)} %get-tuple-element.24.tables, f32[4,512,128]{2,1,0:T(8,128)S(1)} %get-tuple-element.25.gains, f32[512,128]{1,0:T(8,128)S(1)} %bitcast.22, ...), custom_call_target="tpu_custom_call", output_to_operand_aliasing={{0}: (8, {})} | custom-call | tf_op jit(solution)/shard_map/finish/pallas_call | solution.py:496
Async XLA Ops:
  4.4 22.1 %all-to-all-start = ((f32[128,1,384]{2,1,0:T(1,128)}), f32[128,1,384]{2,1,0:T(1,128)S(1)}, u32[]{:S(2)}, u32[]{:S(2)}) async-start(f32[128,1,384]{2,1,0:T(1,128)} %bitcast.10), calls=%async_computation | async-start | bytes 393216 | tf_op jit(solution)/shard_map/all_to_all | solution.py:450
  15.9 10.6 %copy-start.3 = (f32[1,128]{1,0:T(1,128)S(1)}, f32[1,128]{1,0:T(1,128)}, u32[]{:S(2)}) copy-start(f32[1,128]{1,0:T(1,128)} %volume.1) | copy-start | bytes 1540
  15.9 15.9 %copy-start = (f32[65536]{0:T(1024)S(1)}, f32[65536]{0:T(1024)}, u32[]{:S(2)}) copy-start(f32[65536]{0:T(1024)} %param.14) | copy-start | bytes 786436
  15.9 15.9 %copy-start.1 = (s32[65536]{0:T(1024)S(1)}, s32[65536]{0:T(1024)}, u32[]{:S(2)}) copy-start(s32[65536]{0:T(1024)} %param.15) | copy-start | bytes 786436
  15.9 15.9 %copy-start.2 = (f32[65536]{0:T(1024)S(1)}, f32[65536]{0:T(1024)}, u32[]{:S(2)}) copy-start(f32[65536]{0:T(1024)} %param.13) | copy-start | bytes 786436
  27.8 17.5 %all-to-all-start.1 = ((f32[128,1,896]{2,1,0:T(1,128)}), f32[128,1,896]{2,1,0:T(1,128)S(1)}, u32[]{:S(2)}, u32[]{:S(2)}) async-start(f32[128,1,896]{2,1,0:T(1,128)} %bitcast.14), calls=%async_computation.1 | async-start | bytes 917504 | tf_op jit(solution)/shard_map/all_to_all | solution.py:450

commit v4 on v3

--- a/solution.py
+++ b/solution.py
@@ -131,14 +131,24 @@
     send[pl.ds(0, W, AHEAD), :] = got[:, :W] + got[:, W : 2 * W] + got[:, 2 * W :]
 
 
-def soil_kernel(soil, coef, rain, after, owner, reach, soil_mid, mid0, share, hit, spot, water_v, coef_v, out_v, rain_v, sems, out_sems):
+def soil_kernel(
+    soil, coef, rain, after, owner_hbm, reach_hbm, soil_mid, mid0, share, hit, spot,
+    water_v, coef_v, out_v, rain_v, owner, reach, sems, out_sems, small_sems
+):
     del after
+    small = run_all(
+        [
+            pltpu.make_async_copy(owner_hbm, owner, small_sems.at[0]),
+            pltpu.make_async_copy(reach_hbm, reach, small_sems.at[1]),
+        ]
+    )
     layers = water_v.shape[0]
     loads = run_all([pltpu.make_async_copy(rain, rain_v, sems.at[0, layers])])
     for layer in range(layers):
         loads.append(pltpu.make_async_copy(soil.at[:, layer, :], water_v.at[layer], sems.at[0, layer]))
         loads.append(pltpu.make_async_copy(coef.at[:, layer, :], coef_v.at[layer], sems.at[1, layer]))
     run_all(loads[1:])
+    wait_all(small)
     sub = iota((W, W), 0)
     for step in range(owner.shape[0]):
         at = slice(step * CHUNK, (step + 1) * CHUNK)
@@ -280,12 +290,14 @@
     got = recv[pl.ds(0, W, AHEAD), :]
     turned = jnp.transpose(got)
     lane = iota((W, W), 1)
-    total = jnp.zeros((48, W), jnp.float32)
+    hits, parts = [], []
     for c in range(8):
         at = jnp.broadcast_to(got[:, c * 16 + 10 : c * 16 + 11], (W, W)).astype(jnp.int32)
-        hit = (at == lane).astype(jnp.bfloat16)
-        parts = jnp.concatenate(split3(turned[c * 16 : c * 16 + 16, :]), axis=0)
-        total += jnp.dot(parts, hit, preferred_element_type=jnp.float32)
+        hits.append((at == lane).astype(jnp.bfloat16))
+        parts.append(jnp.concatenate(split3(turned[c * 16 : c * 16 + 16, :]), axis=0))
+    total = jnp.dot(
+        jnp.concatenate(parts, axis=1), jnp.concatenate(hits, axis=0), preferred_element_type=jnp.float32
+    )
     total = total[:16, :] + total[16:32, :] + total[32:, :]
     row = lambda f: total[f : f + 1, :]
     vol = volume[...]
@@ -454,7 +466,7 @@
 
     soil_mid, mid0, share, hit, spot = pl.pallas_call(
         soil_kernel,
-        in_specs=[hbm] * 4 + [vmem] * 2,
+        in_specs=[hbm] * 6,
         out_specs=[hbm] + [vmem] * 4,
         out_shape=[
             pltpu.HBM((blocks, layers, W), f32),
@@ -463,7 +475,10 @@
             pltpu.HBM((blocks, W), b16),
             pltpu.HBM((blocks, W), i32),
         ],
-        scratch_shapes=[scratch(f32, layers, blocks, W)] * 3 + [flat(f32), sems(2, layers + 1), sems(layers)],
+        scratch_shapes=[scratch(f32, layers, blocks, W)] * 3
+        + [flat(f32)]
+        + [scratch(i32, steps, CHUNK)] * 2
+        + [sems(2, layers + 1), sems(layers), sems(2)],
         compiler_params=params,
         cost_estimate=cost(3_000_000, 10 * MB),
         name="soil",

time: 48.1 us -> 48.1 us (level)
  no operation moved by 1% of the time
where the time goes in v4:
time: 48.1 us; the launch traced here: 47.8 us
  Pallas kernels  16.5 us (34%)
  starting transfers between devices  15.5 us (32%)
  waiting for transfers between devices  15 us (31%)
  between operations  0.73 us (2%)
    all_to_all x2, starting transfers between devices, exchange(): rows = lax.all_to_all(rows, axes, split_axis=0, concat_axis=0, tiled=True)  15.5 us
    all_to_all x2, waiting for transfers between devices, exchange(): rows = lax.all_to_all(rows, axes, split_axis=0, concat_axis=0, tiled=True)  15 us
    pallas_call x1, Pallas kernels, local(): pl.pallas_call(inflow_kernel, in_specs=[hbm] * 3 + [vmem] * 4, out_specs=...  4.71 us
    pallas_call x1, Pallas kernels, local(): pl.pallas_call(soil_kernel, in_specs=[hbm] * 6, out_specs=[hbm] + [vmem]...  4.16 us
    pallas_call x1, Pallas kernels, local(): pl.pallas_call(moments_kernel, in_specs=[hbm] * 10, out_specs=vmem, out_s...  3.77 us
    pallas_call x1, Pallas kernels, local(): pl.pallas_call(finish_kernel, in_specs=[vmem] * 5 + [hbm] * 4, out_specs=...  2.59 us
    pallas_call x1, Pallas kernels, local(): pl.pallas_call(reach_kernel, in_specs=[vmem] * 2, out_specs=vmem, out_sha...  1.24 us
  transfers between devices with their start and end apart: 2, of which 2 were waited for; matrix products, arithmetic and copies ran while one was open for 0% of the time, Pallas kernels for 19%

profile of v4, /device:TPU:1, one launch (start us, length us, event | category | flops | bytes accessed | tf_op | source)
XLA Modules:
  0.0 47.8 jit_solution(2121154221184163659)
XLA Ops:
  0.6 3.8 %moments.1.after = f32[384,128]{1,0:T(8,128)} custom-call(f32[512,6,128]{2,1,0:T(8,128)} %bitcast.31, f32[512,6,128]{2,1,0:T(8,128)} %bitcast.33, f32[512,128]{1,0:T(8,128)} %bitcast.36, f32[512,128]{1,0:T(8,128)} %bitcast.29, f32[512,128]{1,0:T(8,128)} %bitcast.20, s32[512,128]{1,0:T(8,128)} %bitcast.23, s32[4,128]{1,0:T(4,128)} %bitcast.38, ...), custom_call_target="tpu_custom_call" | custom-call | tf_op jit(solution)/shard_map/moments/pallas_call | solution.py:446
  4.4 11.5 %all-to-all-start = ((f32[128,1,384]{2,1,0:T(1,128)}), f32[128,1,384]{2,1,0:T(1,128)S(1)}, u32[]{:S(2)}, u32[]{:S(2)}) async-start(f32[128,1,384]{2,1,0:T(1,128)} %bitcast.10), calls=%async_computation | async-start | bytes 393216 | tf_op jit(solution)/shard_map/all_to_all | solution.py:462
  15.9 0.0 copy-start.3
  15.9 0.0 copy-start
  15.9 0.0 copy-start.1
  15.9 0.0 copy-start.2
  16.0 4.2 %soil.1 = (f32[512,6,128]{2,1,0:T(8,128)}, f32[512,128]{1,0:T(8,128)}, f32[512,128]{1,0:T(8,128)}, bf16[512,128]{1,0:T(8,128)(2,1)}, s32[512,128]{1,0:T(8,128)}) custom-call(f32[512,6,128]{2,1,0:T(8,128)} %bitcast.32, f32[512,6,128]{2,1,0:T(8,128)} %bitcast.34, f32[512,128]{1,0:T(8,128)} %bitcast.37, f32[384,128]{1,0:T(8,128)} %moments.1.after, ...), custom_call_target="tpu_custom_call" | custom-call | flops 3000000 | bytes 10485760 | tf_op jit(solution)/shard_map/soil/pallas_call | solution.py:467
  20.1 6.4 %all-to-all-done = f32[128,1,384]{2,1,0:T(1,128)S(1)} async-done(((f32[128,1,384]{2,1,0:T(1,128)}), f32[128,1,384]{2,1,0:T(1,128)S(1)}, u32[]{:S(2)}, u32[]{:S(2)}) %all-to-all-start) | async-done | bytes 196640 | tf_op jit(solution)/shard_map/all_to_all | solution.py:462
  26.5 0.0 copy-done.3
  26.5 1.2 %reaches.1 = f32[896,128]{1,0:T(8,128)} custom-call(f32[384,128]{1,0:T(8,128)S(1)} %bitcast.27, f32[1,128]{1,0:T(1,128)S(1)} %copy-done.3), custom_call_target="tpu_custom_call" | custom-call | tf_op jit(solution)/shard_map/reaches/pallas_call | solution.py:489
  27.8 4.0 %all-to-all-start.1 = ((f32[128,1,896]{2,1,0:T(1,128)}), f32[128,1,896]{2,1,0:T(1,128)S(1)}, u32[]{:S(2)}, u32[]{:S(2)}) async-start(f32[128,1,896]{2,1,0:T(1,128)} %bitcast.14), calls=%async_computation.1 | async-start | bytes 917504 | tf_op jit(solution)/shard_map/all_to_all | solution.py:462
  31.8 0.0 copy-done
  31.8 0.0 copy-done.1
  31.8 0.0 copy-done.2
  31.8 4.7 %inflow.1 = (f32[4,512,128]{2,1,0:T(8,128)S(1)}, f32[15,128,128]{2,1,0:T(8,128)S(1)}) custom-call(f32[512,128]{1,0:T(8,128)} %get-tuple-element.20.share, bf16[512,128]{1,0:T(8,128)(2,1)} %get-tuple-element.21.hit, s32[512,128]{1,0:T(8,128)} %get-tuple-element.22.spot, f32[512,128]{1,0:T(8,128)S(1)} %bitcast.30, f32[512,128]{1,0:T(8,128)S(1)} %bitcast.21, ...), custom_call_target="tpu_custom_call" | custom-call | flops 10000000 | bytes 16777216 | tf_op jit(solution)/shard_map/inflow/pallas_call | solution.py:500
  36.6 8.7 %all-to-all-done.1 = f32[128,1,896]{2,1,0:T(1,128)S(1)} async-done(((f32[128,1,896]{2,1,0:T(1,128)}), f32[128,1,896]{2,1,0:T(1,128)S(1)}, u32[]{:S(2)}, u32[]{:S(2)}) %all-to-all-start.1) | async-done | bytes 458784 | tf_op jit(solution)/shard_map/all_to_all | solution.py:462
  45.2 2.6 %finish.1 = (f32[512,6,128]{2,1,0:T(8,128)}, f32[512,128]{1,0:T(8,128)}, f32[1,128]{1,0:T(1,128)}) custom-call(f32[896,128]{1,0:T(8,128)S(1)} %bitcast.26, f32[15,128,128]{2,1,0:T(8,128)S(1)} %get-tuple-element.24.tables, f32[4,512,128]{2,1,0:T(8,128)S(1)} %get-tuple-element.25.gains, f32[512,128]{1,0:T(8,128)S(1)} %bitcast.22, ...), custom_call_target="tpu_custom_call", output_to_operand_aliasing={{0}: (8, {})} | custom-call | tf_op jit(solution)/shard_map/finish/pallas_call | solution.py:511
Async XLA Ops:
  4.4 22.1 %all-to-all-start = ((f32[128,1,384]{2,1,0:T(1,128)}), f32[128,1,384]{2,1,0:T(1,128)S(1)}, u32[]{:S(2)}, u32[]{:S(2)}) async-start(f32[128,1,384]{2,1,0:T(1,128)} %bitcast.10), calls=%async_computation | async-start | bytes 393216 | tf_op jit(solution)/shard_map/all_to_all | solution.py:462
  15.9 10.6 %copy-start.3 = (f32[1,128]{1,0:T(1,128)S(1)}, f32[1,128]{1,0:T(1,128)}, u32[]{:S(2)}) copy-start(f32[1,128]{1,0:T(1,128)} %volume.1) | copy-start | bytes 1540
  15.9 15.9 %copy-start = (f32[65536]{0:T(1024)S(1)}, f32[65536]{0:T(1024)}, u32[]{:S(2)}) copy-start(f32[65536]{0:T(1024)} %param.14) | copy-start | bytes 786436
  15.9 15.9 %copy-start.1 = (s32[65536]{0:T(1024)S(1)}, s32[65536]{0:T(1024)}, u32[]{:S(2)}) copy-start(s32[65536]{0:T(1024)} %param.15) | copy-start | bytes 786436
  15.9 15.9 %copy-start.2 = (f32[65536]{0:T(1024)S(1)}, f32[65536]{0:T(1024)}, u32[]{:S(2)}) copy-start(f32[65536]{0:T(1024)} %param.13) | copy-start | bytes 786436
  27.8 17.5 %all-to-all-start.1 = ((f32[128,1,896]{2,1,0:T(1,128)}), f32[128,1,896]{2,1,0:T(1,128)S(1)}, u32[]{:S(2)}, u32[]{:S(2)}) async-start(f32[128,1,896]{2,1,0:T(1,128)} %bitcast.14), calls=%async_computation.1 | async-start | bytes 917504 | tf_op jit(solution)/shard_map/all_to_all | solution.py:462
